TPU v7x, 256 devices: a whole 4x4x8 slice. The times are simulated.
256 devices in a mesh: seq: 16 (over x, y), dp: 8 (over z), head: 2 (over core).
Axes of the slice: x: 4, y: 4, z: 8, core: 2. Of those that a mesh axis runs over, the one named last changes fastest.
Arguments:
- queries: bfloat16 [8, 4096, 2048], P('dp', 'seq', 'head'), may hold values from -40 to 40
- out_grad: bfloat16 [8, 4096, 2048], P('dp', 'seq', 'head'), may hold values from -96 to 96
- encodings: bfloat16 [8, 16384, 896], P('dp', 'seq'), may hold values from -6 to 6
- owner_map: int32 [8, 64, 2], P('dp', 'seq'), may hold values from 0 to 127, as said below
- nbr_count: int32 [8, 64], P('dp', 'seq'), may hold values from 1 to 2
- key_weight: bfloat16 [896, 2048], P(None, 'head'), may hold values from -1 to 1
- value_weight: bfloat16 [896, 2048], P(None, 'head'), may hold values from -0.1875 to 0.1875
Outputs:
- grad_query: bfloat16 [8, 4096, 2048], P('dp', 'seq', 'head')
- grad_enc: bfloat16 [8, 16384, 896], P('dp', 'seq')
- grad_kv_weight: float32 [896, 2, 2048], P(('seq', 'dp'), None, 'head')
Inputs may be any that keep to these rules, and one draw needn't show every extreme that they name: `owner_map`: an entry e names the neighbour at place e % 8 on the device with index e // 8 along seq that holds the same sequence. Among the 8 references of the spans of one device, each device along seq is named either by none or by exactly 1 of them.
All inputs are finite; a program needn't handle non-finite values.
Results may differ from a plain program's by a relative error of at most 0.023.
The roundings to bfloat16 on the way count: a program that leaves them out, or rounds other values in their place, can miss the bound.
Values may be sent and summed in bfloat16 or wider, within the bound.
A program may use at most 128 MiB of HBM per device.

v0:
```python
import math

import jax
import jax.numpy as jnp
from jax import lax
from jax.sharding import PartitionSpec as P

HD = 128
SPAN = 64
NBR = 2
NROWS = 128


def passed_along(shard, axis, by):
    count = lax.axis_size(axis)
    pairs = [(i, i + by) for i in range(count) if 0 <= i + by < count]
    return lax.ppermute(shard, axis, pairs)


def rank_within(owners):
    order = jnp.arange(owners.shape[0])
    same_owner = owners[:, None] == owners[None, :]
    earlier = order[None, :] < order[:, None]
    return jnp.sum(jnp.logical_and(same_owner, earlier), axis=1)


def body(queries, out_grad, encodings, owner_map, nbr_count, key_weight, value_weight):
    rows_dev = queries.shape[1]
    features = queries.shape[2]
    heads_per_processor = features // HD
    peer_count = lax.axis_size("seq")
    span_count = owner_map.shape[1]
    ref_count = span_count * owner_map.shape[2]
    owned = encodings.shape[1] // NROWS
    slot_cap = max(1, ref_count // peer_count)
    slot_count = peer_count * slot_cap
    rim_rows = SPAN - 1
    score_scale = 1.0 / math.sqrt(HD)
    highest = lax.Precision.HIGHEST
    next_query, next_grad = passed_along((queries[0, :rim_rows], out_grad[0, :rim_rows]), "seq", -1)
    shifted_query = jnp.concatenate([queries[0, rim_rows:], next_query], axis=0)
    shifted_grad = jnp.concatenate([out_grad[0, rim_rows:], next_grad], axis=0)
    targets = owner_map[0].reshape(ref_count)
    owners = targets // owned
    places = targets % owned
    slot_of = owners * slot_cap + rank_within(owners)
    slot_ids = jnp.arange(slot_count)
    asked_ids = (
        jnp.sum(jnp.where(slot_of[None, :] == slot_ids[:, None], places[None, :] + 1, 0), axis=1)
        - 1
    )
    asked_ids = asked_ids.reshape(peer_count, slot_cap)
    wanted = lax.all_to_all(asked_ids, "seq", split_axis=0, concat_axis=0, tiled=True).reshape(
        slot_count
    )
    is_live = wanted >= 0
    picked = jnp.maximum(wanted, 0)
    flat_enc = encodings[0]
    zero_low = jnp.zeros((), jnp.bfloat16)
    own_keys = (
        jnp.dot(flat_enc, key_weight, preferred_element_type=jnp.float32)
        .astype(jnp.bfloat16)
        .reshape(owned, NROWS, features)
    )
    own_values = (
        jnp.dot(flat_enc, value_weight, preferred_element_type=jnp.float32)
        .astype(jnp.bfloat16)
        .reshape(owned, NROWS, features)
    )
    send_keys = jnp.where(is_live[:, None, None], own_keys[picked], zero_low)
    send_values = jnp.where(is_live[:, None, None], own_values[picked], zero_low)
    got_keys, got_values = (
        lax.all_to_all(send_keys, "seq", split_axis=0, concat_axis=0, tiled=True),
        lax.all_to_all(send_values, "seq", split_axis=0, concat_axis=0, tiled=True),
    )
    ref_keys = got_keys[slot_of]
    ref_values = got_values[slot_of]
    context_keys = ref_keys.reshape(span_count, NBR * NROWS, heads_per_processor, HD)
    context_values = ref_values.reshape(span_count, NBR * NROWS, heads_per_processor, HD)
    query_blocks = shifted_query.reshape(span_count, SPAN, heads_per_processor, HD)
    grad_blocks = shifted_grad.reshape(span_count, SPAN, heads_per_processor, HD)
    allowed = (jnp.arange(NBR * NROWS) // NROWS)[None, :] < nbr_count[0][:, None]
    logit_scores = (
        jnp.einsum(
            "cqhd,ckhd->chqk", query_blocks, context_keys, preferred_element_type=jnp.float32
        )
        * score_scale
    )
    logit_scores = jnp.where(allowed[:, None, None, :], logit_scores, -1e30)
    row_max = jnp.max(logit_scores, axis=-1, keepdims=True)
    weights = jnp.exp(logit_scores - row_max)
    softmax_p = weights / jnp.sum(weights, axis=-1, keepdims=True)
    prob_bf = softmax_p.astype(jnp.bfloat16)
    attended = jnp.einsum(
        "chqk,ckhd->cqhd", prob_bf, context_values, preferred_element_type=jnp.float32
    )
    row_delta = jnp.sum(grad_blocks.astype(jnp.float32) * attended, axis=-1)
    dprobs = jnp.einsum(
        "cqhd,ckhd->chqk", grad_blocks, context_values, preferred_element_type=jnp.float32
    )
    dscores = softmax_p * (dprobs - jnp.transpose(row_delta, (0, 2, 1))[..., None])
    dscore_bf = dscores.astype(jnp.bfloat16)
    gradient_offset = (
        jnp.einsum("chqk,ckhd->cqhd", dscore_bf, context_keys, preferred_element_type=jnp.float32)
        * score_scale
    )
    gradient_offset = gradient_offset.astype(jnp.bfloat16).reshape(rows_dev, features)
    ref_key_grad = (
        jnp.einsum("chqk,cqhd->ckhd", dscore_bf, query_blocks, preferred_element_type=jnp.float32)
        * score_scale
    )
    ref_key_grad = ref_key_grad.astype(jnp.bfloat16).reshape(ref_count, NROWS, features)
    ref_value_grad = jnp.einsum(
        "chqk,cqhd->ckhd", prob_bf, grad_blocks, preferred_element_type=jnp.float32
    )
    ref_value_grad = ref_value_grad.astype(jnp.bfloat16).reshape(ref_count, NROWS, features)
    received = passed_along(gradient_offset[rows_dev - rim_rows :], "seq", 1)
    grad_query = jnp.concatenate([received, gradient_offset[: rows_dev - rim_rows]], axis=0)[None]
    select = (wanted[None, :] == jnp.arange(owned)[:, None]).astype(jnp.float32)
    blank_slots = jnp.zeros((slot_count, NROWS, features), jnp.bfloat16)
    got_key_grad, got_value_grad = (
        lax.all_to_all(
            blank_slots.at[slot_of].set(ref_key_grad),
            "seq",
            split_axis=0,
            concat_axis=0,
            tiled=True,
        ),
        lax.all_to_all(
            blank_slots.at[slot_of].set(ref_value_grad),
            "seq",
            split_axis=0,
            concat_axis=0,
            tiled=True,
        ),
    )
    summed_keys = jnp.dot(
        select,
        got_key_grad.reshape(slot_count, NROWS * features).astype(jnp.float32),
        precision=highest,
    )
    summed_keys = summed_keys.reshape(owned * NROWS, features)
    summed_values = jnp.dot(
        select,
        got_value_grad.reshape(slot_count, NROWS * features).astype(jnp.float32),
        precision=highest,
    )
    summed_values = summed_values.reshape(owned * NROWS, features)
    key_wide = key_weight.astype(jnp.float32)
    value_wide = value_weight.astype(jnp.float32)
    enc_partial = jnp.einsum("rf,ef->re", summed_keys, key_wide, precision=highest)
    enc_partial = enc_partial + jnp.einsum(
        "rf,ef->re", summed_values, value_wide, precision=highest
    )
    grad_enc = lax.psum(enc_partial, "head").astype(jnp.bfloat16)[None]
    enc_columns = flat_enc.astype(jnp.float32)
    key_part = jnp.einsum("rc,rf->cf", enc_columns, summed_keys, precision=highest)
    value_part = jnp.einsum("rc,rf->cf", enc_columns, summed_values, precision=highest)
    grad_weight = lax.psum_scatter(
        jnp.stack([key_part, value_part], axis=1), ("seq", "dp"), scatter_dimension=0, tiled=True
    )
    return (grad_query, grad_enc, grad_weight)


def solution(mesh):
    return jax.shard_map(
        body,
        mesh=mesh,
        in_specs=(
            P("dp", "seq", "head"),
            P("dp", "seq", "head"),
            P("dp", "seq", None),
            P("dp", "seq", None),
            P("dp", "seq"),
            P(None, "head"),
            P(None, "head"),
        ),
        out_specs=(P("dp", "seq", "head"), P("dp", "seq", None), P(("seq", "dp"), None, "head")),
        check_vma=False,
    )
```

profile of v0, /device:TPU:1, one launch (start us, length us, event | category | flops | bytes accessed | tf_op | source)
XLA Modules:
  0.0 620.3 jit_solution(18112496786661055170)
XLA Ops:
  7.2 0.9 copy.60
  8.2 0.2 convert_reduce_fusion
  8.5 0.7 copy.61
  9.2 7.6 %all-to-all-start = ((s32[16,1,1]{2,1,0:T(1,128)}), s32[16,1,1]{2,1,0:T(1,128)S(1)}, u32[]{:S(2)}, u32[]{:S(2)}) async-start(s32[16,1,1]{2,1,0:T(1,128)} %copy.61), calls=%async_computation | async-start | bytes 16384 | tf_op jit(solution)/shard_map/all_to_all | solution.py:53
  16.8 5.3 convolution_convert_fusion.1
  22.1 3.7 convolution_convert_fusion
  25.8 0.7 fusion.54
  26.5 4.4 gather_fusion
  30.9 4.4 gather_fusion.2
  35.3 0.4 compare_reduce_fusion
  35.7 6.1 broadcast_select_fusion.1
  41.8 54.8 %all_to_all.26 = bf16[16,128,1024]{2,1,0:T(8,128)(2,1)} all-to-all(bf16[16,128,1024]{2,1,0:T(8,128)(2,1)S(1)} %get-tuple-element.11), channel_id=1, replica_groups=mesh['seq'=16,'dp'=8,'head'=2] {'seq'}, dimensions={0} | all-to-all | bytes 8388608 | tf_op jit(solution)/shard_map/all_to_all | solution.py:73
  96.6 5.4 all-to-all-start.2
  102.0 1.3 collective-permute-start.1
  103.4 1.5 collective-permute-start
  105.0 0.1 slice_bitcast_fusion.1
  105.1 0.1 slice_bitcast_fusion
  105.3 47.8 %collective-permute-done = bf16[63,1024]{1,0:T(8,128)(2,1)S(1)} collective-permute-done((bf16[63,1024]{1,0:T(8,128)(2,1)S(1)}, bf16[63,1024]{1,0:T(8,128)(2,1)S(1)}, u32[]{:S(2)}, u32[]{:S(2)}) %collective-permute-start) | collective-permute-done | bytes 129056 | tf_op jit(solution)/shard_map/ppermute | solution.py:17
  153.2 0.1 copy.76
  153.4 4.4 gather_fusion.1
  157.8 3.6 copy.77
  161.4 4.2 gather_fusion.3
  165.6 3.7 copy.79
  169.3 0.8 fusion.2
  170.1 2.0 fusion.55
  172.1 6.1 fusion.29
  178.3 3.2 multiply_convert_fusion.1
  181.5 2.1 fusion.14
  183.6 4.3 copy.72
  187.9 4.2 reshape.323
  192.1 2.6 broadcast_in_dim.74.clone
  194.7 5.8 scatter_fusion
  200.5 11.2 %all-to-all-start.3 = ((bf16[16,128,1024]{2,1,0:T(8,128)(2,1)}), bf16[16,128,1024]{2,1,0:T(8,128)(2,1)}, u32[]{:S(2)}, u32[]{:S(2)}) async-start(bf16[16,128,1024]{2,1,0:T(8,128)(2,1)} %scatter_fusion), calls=%async_computation.3 | async-start | bytes 8388608 | tf_op jit(solution)/shard_map/all_to_all | solution.py:122
  211.7 7.0 %convert_bitcast_fusion = bf16[4,256,8,128]{1,3,2,0:T(8,128)(2,1)} fusion(bf16[4,64,8,128]{3,2,1,0:T(8,128)(2,1)S(1)} %bitcast.116, f32[4,8,64]{2,1,0:T(8,128)S(1)} %get-tuple-element.15, f32[4,8,64,256]{3,2,1,0:T(8,128)} %copy-done.1, pred[4,256]{1,0:T(4,128)(4,1)S(1)} %broadcast_compare_fusion), kind=kOutput, calls=%fused_computation.11 | convolution fusion | flops 137890048 | bytes 4727808 | tf_op jit(solution)/shard_map/chqk,cqhd->ckhd/dot_general | solution.py:113
  218.7 4.3 copy.74
  223.0 4.2 reshape.331
  227.2 2.5 broadcast_in_dim.74.clone.1
  229.7 5.7 scatter_fusion.1
  235.4 22.3 %all-to-all-done.3 = bf16[16,128,1024]{2,1,0:T(8,128)(2,1)} async-done(((bf16[16,128,1024]{2,1,0:T(8,128)(2,1)}), bf16[16,128,1024]{2,1,0:T(8,128)(2,1)}, u32[]{:S(2)}, u32[]{:S(2)}) %all-to-all-start.3) | async-done | bytes 4194336 | tf_op jit(solution)/shard_map/all_to_all | solution.py:122
  257.7 10.4 %all-to-all-start.4 = ((bf16[16,128,1024]{2,1,0:T(8,128)(2,1)}), bf16[16,128,1024]{2,1,0:T(8,128)(2,1)}, u32[]{:S(2)}, u32[]{:S(2)}) async-start(bf16[16,128,1024]{2,1,0:T(8,128)(2,1)} %scatter_fusion.1), calls=%async_computation.4 | async-start | bytes 8388608 | tf_op jit(solution)/shard_map/all_to_all | solution.py:129
  268.1 0.4 all-reduce.4.cloned.1.call-start
  268.5 4.5 copy.81
  273.0 2.7 fusion.44
  275.8 5.0 reshape.283
  280.7 9.7 %convolution_bitcast_fusion.1 = f32[896,1,1024]{0,2,1:T(8,128)} fusion(f32[1024,1024]{1,0:T(8,128)} %reshape.283, bf16[1,1024,896]{2,1,0:T(8,128)(2,1)S(1)} %copy-done), kind=kOutput, calls=%fused_computation.16 | convolution fusion | flops 11274289152 | bytes 9699328 | tf_op jit(solution)/shard_map/rc,rf->cf/dot_general | solution.py:157
  290.5 23.9 %all-to-all-done.4 = bf16[16,128,1024]{2,1,0:T(8,128)(2,1)} async-done(((bf16[16,128,1024]{2,1,0:T(8,128)(2,1)}), bf16[16,128,1024]{2,1,0:T(8,128)(2,1)}, u32[]{:S(2)}, u32[]{:S(2)}) %all-to-all-start.4) | async-done | bytes 4194336 | tf_op jit(solution)/shard_map/all_to_all | solution.py:129
  314.4 4.5 copy.82
  318.9 2.8 fusion.43
  321.7 5.0 reshape.286
  326.6 8.7 %convolution_bitcast_fusion = f32[896,1,1024]{0,2,1:T(8,128)S(1)} fusion(f32[1024,1024]{1,0:T(8,128)} %reshape.286, bf16[1,1024,896]{2,1,0:T(8,128)(2,1)S(1)} %copy-done), kind=kOutput, calls=%fused_computation.15 | convolution fusion | flops 11274289152 | bytes 9699328 | tf_op jit(solution)/shard_map/rc,rf->cf/dot_general | solution.py:158
  335.3 3.4 pad_maximum_fusion
  338.7 12.0 %copy.75 = f32[896,2,1024]{2,1,0:T(2,128)} copy(f32[896,2,1024]{0,2,1:T(8,128)} %pad_maximum_fusion) | data formatting | bytes 14680064 | tf_op jit(solution)/shard_map/stack | solution.py:160
  350.8 2.1 fusion.32
  352.8 0.3 copy.70
  353.2 0.1 copy.115
  353.3 4.3 collective-permute-start.2
  357.7 0.6 dynamic-slice
  358.9 0.6 collective-permute-done.2
  359.6 0.9 maximum_bitcast_fusion.2
  360.5 9.2 %fusion.56 = f32[1024,896]{1,0:T(8,128)S(1)} fusion(f32[1024,1024]{1,0:T(8,128)} %reshape.283, bf16[896,1024]{1,0:T(8,128)(2,1)} %param.12), kind=kOutput, calls=%fused_computation.96 | convolution fusion | flops 11274289152 | bytes 9699328 | tf_op jit(solution)/shard_map/rf,ef->re/dot_general | solution.py:151
  369.7 8.7 %convolution_add_fusion = f32[1024,896]{1,0:T(8,128)} fusion(f32[1024,896]{1,0:T(8,128)S(1)} %fusion.56, f32[1024,1024]{1,0:T(8,128)S(1)} %copy-done.3, bf16[896,1024]{1,0:T(8,128)(2,1)S(1)} %copy-done.11), kind=kOutput, calls=%fused_computation.33 | convolution fusion | flops 11275206656 | bytes 13369344 | tf_op jit(solution)/shard_map/rf,ef->re/dot_general | solution.py:152
  378.4 21.1 %all-reduce.5 = bf16[1024,896]{1,0:T(8,128)(2,1)} all-reduce(f32[1024,896]{1,0:T(8,128)} %convolution_add_fusion), channel_id=1, replica_groups=mesh['seq'=16,'dp'=8,'head'=2] {'head'}, use_global_device_ids=true, to_apply=%region_7.8 | all-reduce | flops 917504 | bytes 5505024 | tf_op jit(solution)/shard_map/psum | solution.py:155
  399.5 212.4 %all-reduce.4.cloned.1.call-done = f32[896,2,1024]{2,1,0:T(2,128)} async-done(((f32[896,2,1024]{2,1,0:T(2,128)}), f32[896,2,1024]{2,1,0:T(2,128)}) %all-reduce.4.cloned.1.call-update) | async-done | bytes 7340048
  611.8 1.4 constant_dynamic-slice_fusion
  (48 shorter events, 0.8 us)
Async XLA Ops:
  7.2 9.6 %copy-start = (bf16[1,1024,896]{2,1,0:T(8,128)(2,1)S(1)}, bf16[1,1024,896]{2,1,0:T(8,128)(2,1)}, u32[]{:S(2)}) copy-start(bf16[1,1024,896]{2,1,0:T(8,128)(2,1)} %param.9) | copy-start | bytes 5505028
  9.2 16.6 %all-to-all-start = ((s32[16,1,1]{2,1,0:T(1,128)}), s32[16,1,1]{2,1,0:T(1,128)S(1)}, u32[]{:S(2)}, u32[]{:S(2)}) async-start(s32[16,1,1]{2,1,0:T(1,128)} %copy.61), calls=%async_computation | async-start | bytes 16384 | tf_op jit(solution)/shard_map/all_to_all | solution.py:53
  16.8 5.3 copy-start.10
  96.6 5.4 copy-start.6
  96.6 6.7 %copy-start.5 = (bf16[1,256,1024]{2,1,0:T(8,128)(2,1)S(1)}, bf16[1,256,1024]{2,1,0:T(8,128)(2,1)}, u32[]{:S(2)}) copy-start(bf16[1,256,1024]{2,1,0:T(8,128)(2,1)} %param.7) | copy-start | bytes 1572868
  96.6 8.3 %copy-start.9 = (s32[1,4]{1,0:T(1,128)S(1)}, s32[1,4]{1,0:T(1,128)}, u32[]{:S(2)}) copy-start(s32[1,4]{1,0:T(1,128)} %param.11) | copy-start | bytes 52
  96.6 64.8 %all-to-all-start.2 = ((bf16[16,128,1024]{2,1,0:T(8,128)(2,1)}), bf16[16,128,1024]{2,1,0:T(8,128)(2,1)}, u32[]{:S(2)}, u32[]{:S(2)}) async-start(bf16[16,128,1024]{2,1,0:T(8,128)(2,1)} %get-tuple-element.12), calls=%async_computation.2 | async-start | bytes 8388608 | tf_op jit(solution)/shard_map/all_to_all | solution.py:74
  102.0 51.2 %collective-permute-start.1 = (bf16[63,1024]{1,0:T(8,128)(2,1)S(1)}, bf16[63,1024]{1,0:T(8,128)(2,1)S(1)}, u32[]{:S(2)}, u32[]{:S(2)}) collective-permute-start(bf16[63,1024]{1,0:T(8,128)(2,1)S(1)} %slice_bitcast_fusion.2), channel_id=1, source_target_pairs={{16,0},{32,16},{48,32},{64,48},{80,64},{96,80},{112,96},{128,112},... | collective-permute-start | bytes 387080 | tf_op jit(solution)/shard_map/ppermute | solution.py:17
  103.4 49.7 %collective-permute-start = (bf16[63,1024]{1,0:T(8,128)(2,1)S(1)}, bf16[63,1024]{1,0:T(8,128)(2,1)S(1)}, u32[]{:S(2)}, u32[]{:S(2)}) collective-permute-start(bf16[63,1024]{1,0:T(8,128)(2,1)S(1)} %slice_bitcast_fusion.3), channel_id=1, source_target_pairs={{16,0},{32,16},{48,32},{64,48},{80,64},{96,80},{112,96},{128,112},... | collective-permute-start | bytes 387080 | tf_op jit(solution)/shard_map/ppermute | solution.py:17
  153.4 18.7 %copy-start.7 = (bf16[32,8,8,128]{3,2,1,0:T(8,128)(2,1)}, bf16[32,8,8,128]{3,2,1,0:T(8,128)(2,1)S(1)}, u32[]{:S(2)}) copy-start(bf16[32,8,8,128]{3,2,1,0:T(8,128)(2,1)S(1)} %copy.78) | copy-start | bytes 1572868
  165.6 3.7 copy-start.2
  170.1 2.0 copy-start.1
  200.5 11.2 %copy-start.8 = (bf16[32,8,8,128]{3,2,1,0:T(8,128)(2,1)S(1)}, bf16[32,8,8,128]{3,2,1,0:T(8,128)(2,1)}, u32[]{:S(2)}) copy-start(bf16[32,8,8,128]{3,2,1,0:T(8,128)(2,1)} %copy-done.7) | copy-start | bytes 1572868
  200.5 57.2 %all-to-all-start.3 = ((bf16[16,128,1024]{2,1,0:T(8,128)(2,1)}), bf16[16,128,1024]{2,1,0:T(8,128)(2,1)}, u32[]{:S(2)}, u32[]{:S(2)}) async-start(bf16[16,128,1024]{2,1,0:T(8,128)(2,1)} %scatter_fusion), calls=%async_computation.3 | async-start | bytes 8388608 | tf_op jit(solution)/shard_map/all_to_all | solution.py:122
  257.7 56.7 %all-to-all-start.4 = ((bf16[16,128,1024]{2,1,0:T(8,128)(2,1)}), bf16[16,128,1024]{2,1,0:T(8,128)(2,1)}, u32[]{:S(2)}, u32[]{:S(2)}) async-start(bf16[16,128,1024]{2,1,0:T(8,128)(2,1)} %scatter_fusion.1), calls=%async_computation.4 | async-start | bytes 8388608 | tf_op jit(solution)/shard_map/all_to_all | solution.py:129
  268.1 343.8 %all-reduce.4.cloned.1.call-start = ((), (), s32[]{:S(2)}) async-start(), calls=%async_computation.5 | async-start | bytes 14680064
  326.6 8.7 %copy-start.4 = (f32[896,1,1024]{0,2,1:T(8,128)S(1)}, f32[896,1,1024]{0,2,1:T(8,128)}, u32[]{:S(2)}) copy-start(f32[896,1,1024]{0,2,1:T(8,128)} %convolution_bitcast_fusion.1) | copy-start | bytes 11010052
  352.8 4.8 copy-start.12
  353.3 6.2 %collective-permute-start.2 = (bf16[63,1024]{1,0:T(8,128)(2,1)S(1)}, bf16[63,1024]{1,0:T(8,128)(2,1)S(1)}, u32[]{:S(2)}, u32[]{:S(2)}) collective-permute-start(bf16[63,1024]{1,0:T(8,128)(2,1)S(1)} %slice.32), channel_id=1, source_target_pairs={{0,16},{16,32},{32,48},{48,64},{64,80},{80,96},{96,112},{112,128},... | collective-permute-start | bytes 387080 | tf_op jit(solution)/shard_map/ppermute | solution.py:17
  360.5 9.3 %copy-start.3 = (f32[1024,1024]{1,0:T(8,128)S(1)}, f32[1024,1024]{1,0:T(8,128)}, u32[]{:S(2)}) copy-start(f32[1024,1024]{1,0:T(8,128)} %reshape.286) | copy-start | bytes 12582916
  360.5 9.3 %copy-start.11 = (bf16[896,1024]{1,0:T(8,128)(2,1)S(1)}, bf16[896,1024]{1,0:T(8,128)(2,1)}, u32[]{:S(2)}) copy-start(bf16[896,1024]{1,0:T(8,128)(2,1)} %param.13) | copy-start | bytes 5505028
Sparse Core Ops, SparseCore 0:
  350.9 260.9 all-reduce.3
where the time goes:
time: 627 us; the launch traced here: 620 us
  waiting for transfers between devices  307 us (49%)
  local copies, waits for them, and re-layouts  94 us (15%)
  blocking collectives  75.9 us (12%)
  matrix products  72.2 us (12%)
  starting transfers between devices  42 us (7%)
  between operations  15.2 us (2%)
  other arithmetic  13.9 us (2%)
    unnamed x2, waiting for transfers between devices  212 us
    all_to_all x1, blocking collectives, body(): lax.all_to_all(send_keys, 'seq', split_axis=0, concat_axis=0, tiled=True)  54.8 us
    ppermute x3, waiting for transfers between devices, passed_along(): return lax.ppermute(shard, axis, pairs)  48.5 us
    all_to_all x1, waiting for transfers between devices, body(): lax.all_to_all(blank_slots.at[slot_of].set(ref_value_grad), 'seq', split_...  23.9 us
    all_to_all x1, waiting for transfers between devices, body(): lax.all_to_all(blank_slots.at[slot_of].set(ref_key_grad), 'seq', split_ax...  22.3 us
    psum x1, blocking collectives, body(): grad_enc = lax.psum(enc_partial, 'head').astype(jnp.bfloat16)[None]  21.1 us
    unnamed x36, local copies, waits for them, and re-layouts  19.5 us
  transfers between devices with their start and end apart: 8, of which 5 were waited for; matrix products, arithmetic and copies ran while one was open for 14% of the time, Pallas kernels for 0%

commit v1 on v0

v1 whole, which is shorter than its diff:
```python
import functools
import math

import jax
import jax.numpy as jnp
from jax import lax
from jax.experimental import pallas as pl
from jax.experimental.pallas import tpu as pltpu
from jax.sharding import PartitionSpec as P

MESH = pl.DeviceIdType.MESH
HD = 128
SPAN = 64
NROWS = 128
REFS = 8
SIDE = 4
PEERS = SIDE * SIDE
DEPTH = 8
HALF = NROWS // 2
OWNED = 8
D_ENC = 896
FEAT = 1024
ROWS = 256
RIM = 64
STEP = 256
VMEM_LIMIT = 58 << 20
BF = jnp.bfloat16
F32 = jnp.float32


def ring(step):
    return min(step, SIDE - step)


STEPS = sorted(
    [(dx, dy) for dx in range(SIDE) for dy in range(SIDE) if (dx, dy) != (0, 0)],
    key=lambda s: -(ring(s[0]) + ring(s[1])),
)


def plane_place():
    me = lax.axis_index("seq")
    return me, lax.div(me, SIDE), lax.rem(me, SIDE)


def shifted_peer(x, y, dx, dy):
    return lax.rem(x + dx, SIDE) * SIDE + lax.rem(y + dy, SIDE)


def remote(src, dst, send_sem, recv_sem, **where):
    return pltpu.make_async_remote_copy(
        src_ref=src,
        dst_ref=dst,
        send_sem=send_sem,
        recv_sem=recv_sem,
        device_id=where,
        device_id_type=MESH,
    )


def greet(barrier, **where):
    pl.semaphore_signal(barrier, inc=1, device_id=where, device_id_type=MESH)


def nt(a, b):
    return lax.dot_general(a, b, (((1,), (1,)), ((), ())), preferred_element_type=F32)


def tn(a, b):
    return lax.dot_general(a, b, (((0,), (0,)), ((), ())), preferred_element_type=F32)


def nn(a, b):
    return jnp.dot(a, b, preferred_element_type=F32)


def shift_matrix(rows, columns, by):
    i = lax.broadcasted_iota(jnp.int32, (rows, columns), 0)
    e = lax.broadcasted_iota(jnp.int32, (rows, columns), 1)
    return (e == i + by).astype(F32).astype(BF)


def fetch_kernel(
    map_ref, enc_ref, q_ref, d_ref,
    slots_ref, hq_ref, hd_ref, tab_ref,
    asked, tabv, send, isend, irecv, ssend, srecv, fsend, frecv, hsend, hrecv, lsem,
):
    me, x, y = plane_place()
    core = lax.axis_index("head")
    other = 1 - core
    barrier = pltpu.get_barrier_semaphore()
    for dx, dy in STEPS:
        greet(barrier, seq=shifted_peer(x, y, dx, dy))
    greet(barrier, head=other)
    lane = lax.broadcasted_iota(jnp.int32, (1, 128), 1)
    row = jnp.zeros((1, 128), jnp.int32)
    for r in range(REFS):
        entry = map_ref[r // 2, r % 2]
        row = jnp.where(lane == entry // OWNED, entry % OWNED + 1, row)
    asked[...] = row
    tabv[me] = row
    pl.semaphore_wait(barrier, PEERS)

    copies = []
    for k, (dx, dy) in enumerate(STEPS):
        c = remote(asked, tabv.at[me], isend.at[k], irecv.at[k], seq=shifted_peer(x, y, dx, dy))
        c.start()
        copies.append(c)
    before = lax.rem(me + PEERS - 1, PEERS)
    halos = [
        remote(q_ref.at[pl.ds(0, RIM)], hq_ref, hsend.at[0], hrecv.at[0], seq=before),
        remote(d_ref.at[pl.ds(0, RIM)], hd_ref, hsend.at[1], hrecv.at[1], seq=before),
    ]
    for c in copies:
        c.wait_recv()
    lc = pltpu.make_async_copy(tabv, tab_ref, lsem)
    lc.start()
    lc.wait()
    mine = pl.ds(pl.multiple_of(core * HALF, HALF), HALF)
    sends = []
    for k, (dx, dy) in enumerate(STEPS):
        peer = shifted_peer(x, y, dx, dy)
        place = jnp.maximum(tab_ref[peer, 0, me] - 1, 0)
        send[k] = enc_ref[place, mine, :]
        c = remote(send.at[k], slots_ref.at[me, mine], ssend.at[k], srecv.at[k], seq=peer)
        c.start()
        sends.append(c)
    for c in halos:
        c.start()
    slots_ref[me] = enc_ref[jnp.maximum(tab_ref[me, 0, me] - 1, 0)]
    shares = []
    for k in reversed(range(len(STEPS))):
        dx, dy = STEPS[k]
        source = shifted_peer(x, y, SIDE - dx, SIDE - dy)
        sends[k].wait_recv()
        half = slots_ref.at[source, mine]
        c = remote(half, half, fsend.at[k], frecv.at[k], head=other)
        c.start()
        shares.append(c)
    for c in copies:
        c.wait_send()
    for c in halos:
        c.wait()
    for c in sends:
        c.wait_send()
    for c in shares:
        c.wait()


def span_kernel(
    map_ref, cnt_ref, slots_ref, wk_ref, wv_ref, q_ref, d_ref, hq_ref, hd_ref,
    gs_ref, dw_ref, con_ref,
    refs, refs_t, kbuf, vbuf, dkbuf, dvbuf,
):
    scale = 1.0 / math.sqrt(HD)
    step = pl.program_id(0)
    last = lax.axis_index("seq") == PEERS - 1

    @pl.when(step == 0)
    def _():
        for r in range(REFS):
            block = slots_ref[map_ref[r // 2, r % 2] // OWNED]
            refs[pl.ds(r * NROWS, NROWS), :] = block
            refs_t[:, pl.ds(r * NROWS, NROWS)] = block.T
        con_ref[...] = jnp.zeros_like(con_ref)

    wk = wk_ref[...]
    wv = wv_ref[...]
    kbuf[...] = nn(refs[...], wk).astype(BF)
    vbuf[...] = nn(refs[...], wv).astype(BF)
    move = shift_matrix(ROWS, ROWS + RIM, RIM - 1)
    keep = jnp.where(last, 0.0, 1.0).astype(BF)
    qs = nn(move, jnp.concatenate([q_ref[...], hq_ref[...] * keep], axis=0)).astype(BF)
    do = nn(move, jnp.concatenate([d_ref[...], hd_ref[...] * keep], axis=0)).astype(BF)
    col = lax.broadcasted_iota(jnp.int32, (SPAN, 2 * NROWS), 1)
    units = [(c, h) for c in range(REFS // 2) for h in range(STEP // HD)]

    def cut(a, c, h, n):
        return a[c * n : (c + 1) * n, h * HD : (h + 1) * HD]

    keys = [kbuf[pl.ds(c * 2 * NROWS, 2 * NROWS), pl.ds(h * HD, HD)] for c, h in units]
    vals = [vbuf[pl.ds(c * 2 * NROWS, 2 * NROWS), pl.ds(h * HD, HD)] for c, h in units]
    q_u = [cut(qs, c, h, SPAN) for c, h in units]
    d_u = [cut(do, c, h, SPAN) for c, h in units]
    scores = [nt(q, k) * scale for q, k in zip(q_u, keys)]
    dprobs = [nt(d, v) for d, v in zip(d_u, vals)]
    probs, probs_b, ds_b = [], [], []
    for (c, h), s, dp in zip(units, scores, dprobs):
        s = jnp.where(col < cnt_ref[0, c] * NROWS, s, -1e30)
        w = jnp.exp(s - jnp.max(s, axis=-1, keepdims=True))
        p = w / jnp.sum(w, axis=-1, keepdims=True)
        pb = p.astype(BF)
        delta = jnp.sum(pb.astype(F32) * dp, axis=-1, keepdims=True)
        probs_b.append(pb)
        ds_b.append((p * (dp - delta)).astype(BF))
    for (c, h), q, d, k, pb, ds in zip(units, q_u, d_u, keys, probs_b, ds_b):
        at = (pl.ds(c * 2 * NROWS, 2 * NROWS), pl.ds(h * HD, HD))
        gs_ref[pl.ds(c * SPAN, SPAN), pl.ds(h * HD, HD)] = (nn(ds, k) * scale).astype(BF)
        dkbuf[at] = (tn(ds, q) * scale).astype(BF)
        dvbuf[at] = tn(pb, d).astype(BF)
    dw_ref[0] = nn(refs_t[...], dkbuf[...]).astype(BF).reshape(PEERS, D_ENC // PEERS, STEP)
    dw_ref[1] = nn(refs_t[...], dvbuf[...]).astype(BF).reshape(PEERS, D_ENC // PEERS, STEP)
    con_ref[...] += nt(dkbuf[...], wk) + nt(dvbuf[...], wv)


def give_kernel(
    map_ref, tab_ref, con_ref, dw_ref, gs_ref,
    gq_ref, ge_ref, gw_ref,
    hbuf, half, send, recv, ohalf, prev, r1a, r1b, s2a, s2b, r2a, r2b, s3, r3,
    hsem, ssend, srecv, osem, psem, send1a, recv1a, send1b, recv1b,
    send2a, recv2a, send2b, recv2b, send3, recv3,
):
    me, x, y = plane_place()
    core = lax.axis_index("head")
    level = lax.axis_index("dp")
    other = 1 - core
    barrier = pltpu.get_barrier_semaphore()
    for dx, dy in STEPS:
        greet(barrier, seq=shifted_peer(x, y, dx, dy))
    greet(barrier, head=other)
    for dz in range(1, DEPTH):
        greet(barrier, dp=lax.rem(level + dz, DEPTH))
    pl.semaphore_wait(barrier, PEERS + DEPTH - 1)

    mine = pl.ds(pl.multiple_of(core * HALF, HALF), HALF)
    theirs = pl.ds(pl.multiple_of(other * HALF, HALF), HALF)
    swap = remote(con_ref.at[:, theirs], hbuf, hsem.at[0], hsem.at[1], head=other)
    swap.start()
    after = lax.rem(me + 1, PEERS)
    halo = remote(gs_ref.at[pl.ds(ROWS - RIM, RIM)], prev, psem.at[0], psem.at[1], seq=after)
    halo.start()
    first_a, first_b = [], []
    for k in (2, 1, 3):
        xp = lax.rem(x + k, SIDE)
        yp = lax.rem(y + k, SIDE)
        ca = remote(dw_ref.at[0, xp], r1a.at[k - 1], send1a.at[k - 1], recv1a.at[k - 1], seq=xp * SIDE + y)
        cb = remote(dw_ref.at[1, :, yp], r1b.at[k - 1], send1b.at[k - 1], recv1b.at[k - 1], seq=x * SIDE + yp)
        ca.start()
        cb.start()
        first_a.append(ca)
        first_b.append(cb)

    swap.wait()
    for r in range(REFS):
        half[r] = (con_ref[r, mine, :] + hbuf[r]).astype(BF)
    owners = [map_ref[r // 2, r % 2] // OWNED for r in range(REFS)]

    def ref_for(peer):
        found = jnp.int32(0)
        for r in range(REFS):
            found = jnp.where(owners[r] == peer, jnp.int32(r), found)
        return found

    sends = []
    for k, (dx, dy) in enumerate(STEPS):
        peer = shifted_peer(x, y, dx, dy)
        send[k] = half[ref_for(peer)]
        c = remote(send.at[k], recv.at[me], ssend.at[k], srecv.at[k], seq=peer)
        c.start()
        sends.append(c)
    recv[me] = half[ref_for(me)]

    for c in first_a:
        c.wait()
    for c in first_b:
        c.wait()

    def up(a):
        return a.astype(F32)

    for j in range(SIDE):
        s2a[j] = (up(dw_ref[0, x, j]) + up(r1a[0, j]) + up(r1a[1, j]) + up(r1a[2, j])).astype(BF)
        s2b[j] = (up(dw_ref[1, j, y]) + up(r1b[0, j]) + up(r1b[1, j]) + up(r1b[2, j])).astype(BF)
    second = []
    for k in (2, 1, 3):
        xp = lax.rem(x + k, SIDE)
        yp = lax.rem(y + k, SIDE)
        ca = remote(s2a.at[yp], r2a.at[k - 1], send2a.at[k - 1], recv2a.at[k - 1], seq=x * SIDE + yp)
        cb = remote(s2b.at[xp], r2b.at[k - 1], send2b.at[k - 1], recv2b.at[k - 1], seq=xp * SIDE + y)
        ca.start()
        cb.start()
        second += [ca, cb]

    halo.wait()
    old = jnp.where(me == 0, 0.0, 1.0).astype(BF)
    move = shift_matrix(ROWS, ROWS + RIM, 1)
    gq_ref[...] = nn(move, jnp.concatenate([prev[...] * old, gs_ref[...]], axis=0)).astype(BF)

    for c in second:
        c.wait()
    own_a = up(dw_ref[0, x, y]) + up(r1a[0, y]) + up(r1a[1, y]) + up(r1a[2, y])
    own_b = up(dw_ref[1, x, y]) + up(r1b[0, x]) + up(r1b[1, x]) + up(r1b[2, x])
    t_a = (own_a + up(r2a[0]) + up(r2a[1]) + up(r2a[2])).astype(BF)
    t_b = (own_b + up(r2b[0]) + up(r2b[1]) + up(r2b[2])).astype(BF)
    rows = D_ENC // PEERS
    piece = rows // DEPTH
    m = lax.broadcasted_iota(jnp.int32, (DEPTH * 8, rows), 0)
    e = lax.broadcasted_iota(jnp.int32, (DEPTH * 8, rows), 1)
    spread = jnp.logical_and(m // 8 * piece + m % 8 == e, m % 8 < piece).astype(F32).astype(BF)
    s3[:, 0] = nn(spread, t_a).astype(BF).reshape(DEPTH, 8, FEAT)
    s3[:, 1] = nn(spread, t_b).astype(BF).reshape(DEPTH, 8, FEAT)
    third = []
    for dz in (4, 3, 5, 2, 6, 1, 7):
        zp = lax.rem(level + dz, DEPTH)
        c = remote(s3.at[zp], r3.at[dz - 1], send3.at[dz - 1], recv3.at[dz - 1], dp=zp)
        c.start()
        third.append(c)

    for c in sends:
        c.wait()
    row = lax.broadcasted_iota(jnp.int32, (OWNED * HALF, 2 * HALF), 0)
    lane = lax.broadcasted_iota(jnp.int32, (OWNED * HALF, 2 * HALF), 1)
    pick = []
    for t in range(PEERS // 2):
        lo = (tab_ref[2 * t, 0, me] - 1) * HALF
        hi = (tab_ref[2 * t + 1, 0, me] - 1) * HALF
        target = jnp.where(lane < HALF, lane + lo, lane - HALF + hi)
        live = jnp.where(lane < HALF, lo, hi) >= 0
        pick.append(jnp.logical_and(row == target, live).astype(F32).astype(BF))
    total = nn(jnp.concatenate(pick, axis=1), recv[...].reshape(PEERS * HALF, D_ENC))
    total = total.astype(BF).reshape(OWNED, HALF, D_ENC)
    ohalf[...] = total
    ge_ref[:, mine, :] = total
    back = remote(ohalf, ge_ref.at[:, mine], osem.at[0], osem.at[1], head=other)
    back.start()

    for c in third:
        c.wait()
    final = up(s3[level])
    for k in range(DEPTH - 1):
        final = final + up(r3[k])
    gw_ref[:, 0, :] = final[0, :piece]
    gw_ref[:, 1, :] = final[1, :piece]
    back.wait()


def body(queries, out_grad, encodings, owner_map, nbr_count, key_weight, value_weight):
    vm = pl.BlockSpec(memory_space=pltpu.VMEM)
    sm = pl.BlockSpec(memory_space=pltpu.SMEM)
    dma = pltpu.SemaphoreType.DMA
    n = len(STEPS)
    enc = encodings.reshape(OWNED, NROWS, D_ENC)
    q, d = queries[0], out_grad[0]
    slots, hq, hd, tab = pl.pallas_call(
        fetch_kernel,
        out_shape=(
            jax.ShapeDtypeStruct((PEERS, NROWS, D_ENC), BF),
            jax.ShapeDtypeStruct((RIM, FEAT), BF),
            jax.ShapeDtypeStruct((RIM, FEAT), BF),
            jax.ShapeDtypeStruct((PEERS, 1, 128), jnp.int32),
        ),
        in_specs=[sm, vm, vm, vm],
        out_specs=(vm, vm, vm, sm),
        scratch_shapes=[
            pltpu.VMEM((1, 128), jnp.int32),
            pltpu.VMEM((PEERS, 1, 128), jnp.int32),
            pltpu.VMEM((n, HALF, D_ENC), BF),
            dma((n,)), dma((n,)), dma((n,)), dma((n,)), dma((n,)), dma((n,)),
            dma((2,)), dma((2,)), dma,
        ],
        compiler_params=pltpu.CompilerParams(
            collective_id=0, has_side_effects=True, vmem_limit_bytes=VMEM_LIMIT
        ),
        name="fetch",
    )(owner_map[0], enc, q, d)

    rows = D_ENC // PEERS
    gs, dw, con = pl.pallas_call(
        span_kernel,
        grid=(FEAT // STEP,),
        out_shape=(
            jax.ShapeDtypeStruct((ROWS, FEAT), BF),
            jax.ShapeDtypeStruct((2, PEERS, rows, FEAT), BF),
            jax.ShapeDtypeStruct((REFS * NROWS, D_ENC), F32),
        ),
        in_specs=[
            sm, sm,
            pl.BlockSpec((PEERS, NROWS, D_ENC), lambda g: (0, 0, 0)),
            pl.BlockSpec((D_ENC, STEP), lambda g: (0, g)),
            pl.BlockSpec((D_ENC, STEP), lambda g: (0, g)),
            pl.BlockSpec((ROWS, STEP), lambda g: (0, g)),
            pl.BlockSpec((ROWS, STEP), lambda g: (0, g)),
            pl.BlockSpec((RIM, STEP), lambda g: (0, g)),
            pl.BlockSpec((RIM, STEP), lambda g: (0, g)),
        ],
        out_specs=(
            pl.BlockSpec((ROWS, STEP), lambda g: (0, g)),
            pl.BlockSpec((2, PEERS, rows, STEP), lambda g: (0, 0, 0, g)),
            pl.BlockSpec((REFS * NROWS, D_ENC), lambda g: (0, 0)),
        ),
        scratch_shapes=[
            pltpu.VMEM((REFS * NROWS, D_ENC), BF),
            pltpu.VMEM((D_ENC, REFS * NROWS), BF),
            pltpu.VMEM((REFS * NROWS, STEP), BF),
            pltpu.VMEM((REFS * NROWS, STEP), BF),
            pltpu.VMEM((REFS * NROWS, STEP), BF),
            pltpu.VMEM((REFS * NROWS, STEP), BF),
        ],
        compiler_params=pltpu.CompilerParams(
            dimension_semantics=("arbitrary",), vmem_limit_bytes=VMEM_LIMIT
        ),
        name="spans",
    )(owner_map[0], nbr_count, slots, key_weight, value_weight, q, d, hq, hd)

    gq, ge, gw = pl.pallas_call(
        give_kernel,
        out_shape=(
            jax.ShapeDtypeStruct((ROWS, FEAT), BF),
            jax.ShapeDtypeStruct((OWNED, NROWS, D_ENC), BF),
            jax.ShapeDtypeStruct((rows // DEPTH, 2, FEAT), F32),
        ),
        in_specs=[sm, sm, vm, vm, vm],
        out_specs=(vm, vm, vm),
        scratch_shapes=[
            pltpu.VMEM((REFS, HALF, D_ENC), F32),
            pltpu.VMEM((REFS, HALF, D_ENC), BF),
            pltpu.VMEM((n, HALF, D_ENC), BF),
            pltpu.VMEM((PEERS, HALF, D_ENC), BF),
            pltpu.VMEM((OWNED, HALF, D_ENC), BF),
            pltpu.VMEM((RIM, FEAT), BF),
            pltpu.VMEM((SIDE - 1, SIDE, rows, FEAT), BF),
            pltpu.VMEM((SIDE - 1, SIDE, rows, FEAT), BF),
            pltpu.VMEM((SIDE, rows, FEAT), BF),
            pltpu.VMEM((SIDE, rows, FEAT), BF),
            pltpu.VMEM((SIDE - 1, rows, FEAT), BF),
            pltpu.VMEM((SIDE - 1, rows, FEAT), BF),
            pltpu.VMEM((DEPTH, 2, 8, FEAT), BF),
            pltpu.VMEM((DEPTH - 1, 2, 8, FEAT), BF),
            dma((2,)), dma((n,)), dma((n,)), dma((2,)), dma((2,)),
            dma((3,)), dma((3,)), dma((3,)), dma((3,)),
            dma((3,)), dma((3,)), dma((3,)), dma((3,)),
            dma((DEPTH - 1,)), dma((DEPTH - 1,)),
        ],
        compiler_params=pltpu.CompilerParams(
            collective_id=1, has_side_effects=True, vmem_limit_bytes=VMEM_LIMIT
        ),
        name="give",
    )(
        owner_map[0], tab, con.reshape(REFS, NROWS, D_ENC),
        dw.reshape(2, SIDE, SIDE, rows, FEAT), gs,
    )
    return gq[None], ge.reshape(1, OWNED * NROWS, D_ENC), gw


def solution(mesh):
    return jax.shard_map(
        body,
        mesh=mesh,
        in_specs=(
            P("dp", "seq", "head"),
            P("dp", "seq", "head"),
            P("dp", "seq", None),
            P("dp", "seq", None),
            P("dp", "seq"),
            P(None, "head"),
            P(None, "head"),
        ),
        out_specs=(P("dp", "seq", "head"), P("dp", "seq", None), P(("seq", "dp"), None, "head")),
        check_vma=False,
    )
```

time: 627 us -> 148 us (0.24)
  waiting for transfers between devices: 307 us -> 0 us
  Pallas kernels: 0 us -> 140 us
  local copies, waits for them, and re-layouts: 94 us -> 6.71 us
  blocking collectives: 75.9 us -> 0 us
  matrix products: 72.2 us -> 0 us
  starting transfers between devices: 42 us -> 0 us
  between operations: 15.2 us -> 0.65 us
  other arithmetic: 13.9 us -> 0 us
    unnamed x2 -> x0, waiting for transfers between devices: 212 us -> none
    pallas_call x0 -> x3, Pallas kernels: none -> 140 us  [the longest x1 72.1 us: body(): pl.pallas_call(give_kernel, out_shape=(jax.ShapeDtypeStruct((ROWS, FEAT),...]
    dot_general x14 -> x0, matrix products: 72.2 us -> none  [the longest x1 9.74 us: body(): jnp.einsum('rc,rf->cf', enc_columns, summed_keys, precision=highest)]
    all_to_all x1 -> x0, blocking collectives: 54.8 us -> none  [body(): lax.all_to_all(send_keys, 'seq', split_axis=0, concat_axis=0, tiled=True)]
    ppermute x3 -> x0, waiting for transfers between devices: 48.5 us -> none  [passed_along(): return lax.ppermute(shard, axis, pairs)]
    all_to_all x4 -> x0, waiting for transfers between devices: 46.2 us -> none  [the longest x1 23.9 us: body(): lax.all_to_all(blank_slots.at[slot_of].set(ref_value_grad), 'seq', split_...]
    all_to_all x4 -> x0, starting transfers between devices: 34.5 us -> none  [the longest x1 11.2 us: body(): lax.all_to_all(blank_slots.at[slot_of].set(ref_key_grad), 'seq', split_ax...]
    psum x1 -> x0, blocking collectives: 21.1 us -> none  [body(): grad_enc = lax.psum(enc_partial, 'head').astype(jnp.bfloat16)[None]]
  transfers between devices with their start and end apart: 8 -> 0, of which waited for: 5 -> 0; matrix products, arithmetic and copies ran while one was open for 14% -> 0% of each run, Pallas kernels for 0% -> 0%
where the time goes in v1:
time: 148 us; the launch traced here: 147 us
  Pallas kernels  140 us (95%)
  local copies, waits for them, and re-layouts  6.71 us (5%)
    pallas_call x1, Pallas kernels, body(): pl.pallas_call(give_kernel, out_shape=(jax.ShapeDtypeStruct((ROWS, FEAT),...  72.1 us
    pallas_call x1, Pallas kernels, body(): pl.pallas_call(fetch_kernel, out_shape=(jax.ShapeDtypeStruct((PEERS, NROW...  42.7 us
    pallas_call x1, Pallas kernels, body(): pl.pallas_call(span_kernel, grid=(FEAT // STEP,), out_shape=(jax.ShapeDty...  25.1 us
    unnamed x5, local copies, waits for them, and re-layouts  5.37 us

profile of v1, /device:TPU:1, one launch (start us, length us, event | category | flops | bytes accessed | tf_op | source)
XLA Modules:
  0.0 147.3 jit_solution(7445424284736666758)
XLA Ops:
  0.6 1.3 copy.12.map_ref
  2.0 42.7 %fetch.1 = (bf16[16,128,896]{2,1,0:T(8,128)(2,1)}, bf16[64,1024]{1,0:T(8,128)(2,1)}, bf16[64,1024]{1,0:T(8,128)(2,1)}, s32[16,1,128]{2,1,0:T(1,128)}) custom-call(s32[4,2]{1,0:T(4,128)} %copy.12.map_ref, bf16[8,128,896]{2,1,0:T(8,128)(2,1)} %bitcast.14, bf16[256,1024]{1,0:T(8,128)(2,1)} %bitcast.10, bf16[256,1024]{1,0:T(8,128)(2,1)} %bitcast.12), custom_call_target="tpu_custom_call" | custom-call | tf_op jit(solution)/shard_map/fetch/pallas_call | solution.py:344
  44.7 25.1 %spans.1 = (bf16[256,1024]{1,0:T(8,128)(2,1)}, bf16[2,16,56,1024]{3,2,1,0:T(8,128)(2,1)}, f32[1024,896]{1,0:T(8,128)}) custom-call(s32[4,2]{1,0:T(4,128)} %copy.12.map_ref, s32[1,4]{1,0:T(1,128)} %cnt_ref.1, bf16[16,128,896]{2,1,0:T(8,128)(2,1)} %get-tuple-element.14.slots_ref, bf16[896,1024]{1,0:T(8,128)(2,1)} %wk_ref.1, bf16[896,1024]{1,0:T(8,128)(2,1)} %wv_ref.1, ...), custom_call_target="tpu_custom_call" | custom-call | tf_op jit(solution)/shard_map/spans/pallas_call | solution.py:368
  69.8 72.1 %give.1 = (bf16[256,1024]{1,0:T(8,128)(2,1)}, bf16[8,128,896]{2,1,0:T(8,128)(2,1)}, f32[7,2,1024]{2,1,0:T(2,128)}) custom-call(s32[4,2]{1,0:T(4,128)} %copy.12.map_ref, s32[16,1,128]{2,1,0:T(1,128)} %get-tuple-element.13.tab_ref, f32[8,128,896]{2,1,0:T(8,128)} %bitcast.9, bf16[2,4,4,56,1024]{4,3,2,1,0:T(8,128)(2,1)} %bitcast.8, ...), custom_call_target="tpu_custom_call" | custom-call | tf_op jit(solution)/shard_map/give/pallas_call | solution.py:405
  142.0 1.9 %copy.16 = bf16[1,256,1024]{2,1,0:T(8,128)(2,1)} copy(bf16[1,256,1024]{2,1,0:T(8,128)(2,1)} %bitcast.16) | data formatting | bytes 1048576
  143.8 0.0 copy-start
  143.8 2.9 %copy.17 = bf16[1,1024,896]{2,1,0:T(8,128)(2,1)} copy(bf16[1,1024,896]{2,1,0:T(8,128)(2,1)} %bitcast.15) | data formatting | bytes 3670016
  146.7 0.0 copy-done
  146.7 0.6 copy.18
Async XLA Ops:
  143.8 2.9 %copy-start = (f32[7,2,1024]{2,1,0:T(2,128)S(1)}, f32[7,2,1024]{2,1,0:T(2,128)}, u32[]{:S(2)}) copy-start(f32[7,2,1024]{2,1,0:T(2,128)} %get-tuple-element.28) | copy-start | bytes 172036

commit v2 on v0

v2 whole, which is shorter than its diff:
```python
import functools
import math

import jax
import jax.numpy as jnp
from jax import lax
from jax.experimental import pallas as pl
from jax.experimental.pallas import tpu as pltpu
from jax.sharding import PartitionSpec as P

MESH = pl.DeviceIdType.MESH
HD = 128
SPAN = 64
NROWS = 128
REFS = 8
SIDE = 4
PEERS = SIDE * SIDE
DEPTH = 8
HALF = NROWS // 2
OWNED = 8
D_ENC = 896
FEAT = 1024
ROWS = 256
RIM = 64
STEP = 256
GROUPS = FEAT // STEP
SHARE = D_ENC // PEERS
PIECE = SHARE // DEPTH
VMEM_LIMIT = 58 << 20
BF = jnp.bfloat16
F32 = jnp.float32


def plane_place():
    me = lax.axis_index("seq")
    return me, lax.div(me, SIDE), lax.rem(me, SIDE)


def plane_peer(x, y, k):
    return lax.rem(x + lax.div(k, SIDE), SIDE) * SIDE + lax.rem(y + lax.rem(k, SIDE), SIDE)


def opposite(k):
    return lax.rem(SIDE - lax.div(k, SIDE), SIDE) * SIDE + lax.rem(SIDE - lax.rem(k, SIDE), SIDE)


def each(start, stop, step):
    def one(k, carry):
        step(k)
        return carry

    lax.fori_loop(start, stop, one, 0)


def up(a):
    return a.astype(F32)


def remote(src, dst, send_sem, recv_sem, **where):
    return pltpu.make_async_remote_copy(
        src_ref=src,
        dst_ref=dst,
        send_sem=send_sem,
        recv_sem=recv_sem,
        device_id=where,
        device_id_type=MESH,
    )


def greet(barrier, **where):
    pl.semaphore_signal(barrier, inc=1, device_id=where, device_id_type=MESH)


def nt(a, b):
    return lax.dot_general(a, b, (((1,), (1,)), ((), ())), preferred_element_type=F32)


def tn(a, b):
    return lax.dot_general(a, b, (((0,), (0,)), ((), ())), preferred_element_type=F32)


def nn(a, b):
    return jnp.dot(a, b, preferred_element_type=F32)


def shift_matrix(rows, columns, by):
    i = lax.broadcasted_iota(jnp.int32, (rows, columns), 0)
    e = lax.broadcasted_iota(jnp.int32, (rows, columns), 1)
    return (e == i + by).astype(F32).astype(BF)


def kernel(
    map_ref, cnt_ref, enc_hbm, q_hbm, d_hbm, wk_hbm, wv_hbm,
    gq_hbm, ge_hbm, gw_ref,
    enc, wk, wv, qx, dx, asked, tabv, tab, send, slots, keys, vals, enct, refs_t,
    dk, dv, con, hbuf, half, recv, ohalf, gs, prev, gqv, dw, r1a, r1b, s2a, s2b, r2a, r2b, s3, r3,
    lsem, osem, isend, irecv, ssend, srecv, fsend, frecv, halo_send, halo_recv,
    swap_sem, rsend, rrecv, back_sem, prev_sem,
    send1a, recv1a, send1b, recv1b, send2a, recv2a, send2b, recv2b, send3, recv3,
):
    me, x, y = plane_place()
    core = lax.axis_index("head")
    level = lax.axis_index("dp")
    other = 1 - core
    scale = 1.0 / math.sqrt(HD)
    mine = pl.ds(pl.multiple_of(core * HALF, HALF), HALF)
    theirs = pl.ds(pl.multiple_of(other * HALF, HALF), HALF)

    barrier = pltpu.get_barrier_semaphore()
    each(1, PEERS, lambda k: greet(barrier, seq=plane_peer(x, y, k)))
    greet(barrier, head=other)
    each(1, DEPTH, lambda k: greet(barrier, dp=lax.rem(level + k, DEPTH)))

    enc_load = pltpu.make_async_copy(enc_hbm, enc, lsem.at[0])
    enc_load.start()
    loads = []
    for g in range(GROUPS):
        cols = pl.ds(g * STEP, STEP)
        loads.append(pltpu.make_async_copy(q_hbm.at[:, cols], qx.at[g, pl.ds(0, ROWS)], lsem.at[1 + g]))
        loads.append(pltpu.make_async_copy(d_hbm.at[:, cols], dx.at[g, pl.ds(0, ROWS)], lsem.at[5 + g]))
    weights = []
    for g in range(GROUPS):
        cols = pl.ds(g * STEP, STEP)
        weights.append(pltpu.make_async_copy(wk_hbm.at[:, cols], wk.at[g], lsem.at[9 + g]))
        weights.append(pltpu.make_async_copy(wv_hbm.at[:, cols], wv.at[g], lsem.at[13 + g]))
    for c in loads + weights:
        c.start()

    lane = lax.broadcasted_iota(jnp.int32, (1, 128), 1)
    row = jnp.zeros((1, 128), jnp.int32)
    owners, kin = [], []
    for r in range(REFS):
        entry = map_ref[r // 2, r % 2]
        owner = lax.div(entry, OWNED)
        row = jnp.where(lane == owner, lax.rem(entry, OWNED) + 1, row)
        owners.append(owner)
        kx = lax.rem(x - lax.div(owner, SIDE) + SIDE, SIDE)
        ky = lax.rem(y - lax.rem(owner, SIDE) + SIDE, SIDE)
        kin.append(kx * SIDE + ky)
    asked[...] = row
    tabv[0] = row
    con[...] = jnp.zeros_like(con)
    pl.semaphore_wait(barrier, PEERS + DEPTH - 1)

    def ask(k):
        return remote(asked, tabv.at[k], isend.at[k], irecv.at[k], seq=plane_peer(x, y, k))

    each(1, PEERS, lambda k: ask(k).start())
    each(1, PEERS, lambda k: ask(k).wait_recv())
    lc = pltpu.make_async_copy(tabv, tab, lsem.at[17])
    lc.start()
    enc_load.wait()
    lc.wait()

    def give_rows(k):
        return remote(send.at[k], slots.at[k, mine], ssend.at[k], srecv.at[k], seq=plane_peer(x, y, k))

    def share_rows(k):
        part = slots.at[k, mine]
        return remote(part, part, fsend.at[k], frecv.at[k], head=other)

    def start_rows(k):
        place = jnp.maximum(tab[opposite(k), 0, me] - 1, 0)
        send[k] = enc[place, mine, :]
        give_rows(k).start()

    each(1, PEERS, start_rows)
    for c in loads:
        c.wait()
    before = lax.rem(me + PEERS - 1, PEERS)
    halos = [
        remote(qx.at[:, pl.ds(0, RIM)], qx.at[:, pl.ds(ROWS, RIM)], halo_send.at[0], halo_recv.at[0], seq=before),
        remote(dx.at[:, pl.ds(0, RIM)], dx.at[:, pl.ds(ROWS, RIM)], halo_send.at[1], halo_recv.at[1], seq=before),
    ]
    for c in halos:
        c.start()
    slots[0] = enc[jnp.maximum(tab[0, 0, me] - 1, 0)]
    for c in weights:
        c.wait()

    def project(j):
        block = slots[pl.ds(2 * j, 2)].reshape(2 * NROWS, D_ENC)
        for g in range(GROUPS):
            keys[pl.ds(2 * j, 2), g] = nn(block, wk[g]).astype(BF).reshape(2, NROWS, STEP)
            vals[pl.ds(2 * j, 2), g] = nn(block, wv[g]).astype(BF).reshape(2, NROWS, STEP)
        enct[2 * j] = block[:NROWS].T
        enct[2 * j + 1] = block[NROWS:].T

    def arrive(k):
        give_rows(k).wait_recv()
        share_rows(k).start()

    arrive(1)

    def pair(j):
        @pl.when(j < PEERS // 2 - 1)
        def _():
            arrive(2 * j + 2)
            arrive(2 * j + 3)

        @pl.when(j > 0)
        def _():
            share_rows(2 * j).wait_recv()

        share_rows(2 * j + 1).wait_recv()
        project(j)

    each(0, PEERS // 2, pair)
    for c in halos:
        c.wait()
    for r in range(REFS):
        refs_t[:, pl.ds(r * NROWS, NROWS)] = enct[kin[r]]

    move = shift_matrix(ROWS, ROWS + RIM, RIM - 1)
    inside = lax.broadcasted_iota(jnp.int32, (ROWS, ROWS + RIM), 1) < jnp.where(me == PEERS - 1, ROWS, ROWS + RIM)
    move = jnp.where(inside, up(move), 0.0).astype(BF)
    col = lax.broadcasted_iota(jnp.int32, (SPAN, 2 * NROWS), 1)

    def first_a(g, k):
        xp = lax.rem(x + k, SIDE)
        return remote(dw.at[g, 0, xp], r1a.at[g, k - 1], send1a.at[g, k - 1], recv1a.at[g, k - 1], seq=xp * SIDE + y)

    def first_b(g, k):
        yp = lax.rem(y + k, SIDE)
        return remote(dw.at[g, 1, :, yp], r1b.at[g, k - 1], send1b.at[g, k - 1], recv1b.at[g, k - 1], seq=x * SIDE + yp)

    def group(g):
        qs = nn(move, qx[g]).astype(BF)
        do = nn(move, dx[g]).astype(BF)
        units = [(c, h) for c in range(REFS // 2) for h in range(STEP // HD)]

        def cut(a, c, h):
            return a[c * SPAN : (c + 1) * SPAN, h * HD : (h + 1) * HD]

        def both(a, c, h):
            return jnp.concatenate([a[kin[2 * c + n], g, :, pl.ds(h * HD, HD)] for n in range(2)], axis=0)

        k_u = [both(keys, c, h) for c, h in units]
        v_u = [both(vals, c, h) for c, h in units]
        q_u = [cut(qs, c, h) for c, h in units]
        d_u = [cut(do, c, h) for c, h in units]
        scores = [nt(q, k) * scale for q, k in zip(q_u, k_u)]
        dprobs = [nt(d, v) for d, v in zip(d_u, v_u)]
        probs_b, ds_b = [], []
        for (c, h), s, dp in zip(units, scores, dprobs):
            s = jnp.where(col < cnt_ref[0, c] * NROWS, s, -1e30)
            w = jnp.exp(s - jnp.max(s, axis=-1, keepdims=True))
            p = w / jnp.sum(w, axis=-1, keepdims=True)
            pb = p.astype(BF)
            delta = jnp.sum(up(pb) * dp, axis=-1, keepdims=True)
            probs_b.append(pb)
            ds_b.append((p * (dp - delta)).astype(BF))
        for (c, h), q, d, k, pb, ds in zip(units, q_u, d_u, k_u, probs_b, ds_b):
            at = (g, pl.ds(c * 2 * NROWS, 2 * NROWS), pl.ds(h * HD, HD))
            gs[g, pl.ds(c * SPAN, SPAN), pl.ds(h * HD, HD)] = (nn(ds, k) * scale).astype(BF)
            dk[at] = (tn(ds, q) * scale).astype(BF)
            dv[at] = tn(pb, d).astype(BF)
        dw[g, 0] = nn(refs_t[...], dk[g]).astype(BF).reshape(SIDE, SIDE, SHARE, STEP)
        dw[g, 1] = nn(refs_t[...], dv[g]).astype(BF).reshape(SIDE, SIDE, SHARE, STEP)
        for k in (2, 1, 3):
            first_a(g, k).start()
            first_b(g, k).start()
        more = nt(dk[g], wk[g]) + nt(dv[g], wv[g])
        con[...] += more.reshape(REFS, NROWS, D_ENC)

    each(0, GROUPS, group)

    swap = remote(con.at[:, theirs], hbuf, swap_sem.at[0], swap_sem.at[1], head=other)
    swap.start()
    after = lax.rem(me + 1, PEERS)
    halo = remote(gs.at[:, pl.ds(ROWS - RIM, RIM)], prev, prev_sem.at[0], prev_sem.at[1], seq=after)
    halo.start()
    swap.wait()
    for r in range(REFS):
        half[r] = (con[r, mine, :] + hbuf[r]).astype(BF)

    def ref_for(peer):
        found = jnp.int32(0)
        for r in range(REFS):
            found = jnp.where(owners[r] == peer, jnp.int32(r), found)
        return found

    each(1, PEERS, lambda k: give_rows(k).wait_send())

    def return_rows(k):
        return remote(send.at[k], recv.at[k], rsend.at[k], rrecv.at[k], seq=plane_peer(x, y, k))

    def start_return(k):
        send[k] = half[ref_for(plane_peer(x, y, k))]
        return_rows(k).start()

    each(1, PEERS, start_return)
    recv[0] = half[ref_for(me)]

    def second_a(g, k):
        yp = lax.rem(y + k, SIDE)
        return remote(s2a.at[g, yp], r2a.at[g, k - 1], send2a.at[g, k - 1], recv2a.at[g, k - 1], seq=x * SIDE + yp)

    def second_b(g, k):
        xp = lax.rem(x + k, SIDE)
        return remote(s2b.at[g, xp], r2b.at[g, k - 1], send2b.at[g, k - 1], recv2b.at[g, k - 1], seq=xp * SIDE + y)

    def sum_first(g):
        for k in (1, 2, 3):
            first_a(g, k).wait()
            first_b(g, k).wait()
        for j in range(SIDE):
            s2a[g, j] = (up(dw[g, 0, x, j]) + up(r1a[g, 0, j]) + up(r1a[g, 1, j]) + up(r1a[g, 2, j])).astype(BF)
            s2b[g, j] = (up(dw[g, 1, j, y]) + up(r1b[g, 0, j]) + up(r1b[g, 1, j]) + up(r1b[g, 2, j])).astype(BF)
        for k in (2, 1, 3):
            second_a(g, k).start()
            second_b(g, k).start()

    each(0, GROUPS, sum_first)

    halo.wait()
    old = jnp.where(me == 0, 0.0, 1.0)
    back_move = shift_matrix(ROWS, ROWS + RIM, 1)
    for g in range(GROUPS):
        ext = jnp.concatenate([(up(prev[g]) * old).astype(BF), gs[g]], axis=0)
        gqv[:, pl.ds(g * STEP, STEP)] = nn(back_move, ext).astype(BF)
    gq_out = pltpu.make_async_copy(gqv, gq_hbm, osem.at[0])
    gq_out.start()

    m = lax.broadcasted_iota(jnp.int32, (DEPTH * 8, SHARE), 0)
    e = lax.broadcasted_iota(jnp.int32, (DEPTH * 8, SHARE), 1)
    spread = jnp.logical_and(m // 8 * PIECE + m % 8 == e, m % 8 < PIECE).astype(F32).astype(BF)
    for g in range(GROUPS):
        for k in (1, 2, 3):
            second_a(g, k).wait()
            second_b(g, k).wait()
        own_a = up(dw[g, 0, x, y]) + up(r1a[g, 0, y]) + up(r1a[g, 1, y]) + up(r1a[g, 2, y])
        own_b = up(dw[g, 1, x, y]) + up(r1b[g, 0, x]) + up(r1b[g, 1, x]) + up(r1b[g, 2, x])
        t_a = (own_a + up(r2a[g, 0]) + up(r2a[g, 1]) + up(r2a[g, 2])).astype(BF)
        t_b = (own_b + up(r2b[g, 0]) + up(r2b[g, 1]) + up(r2b[g, 2])).astype(BF)
        cols = pl.ds(g * STEP, STEP)
        s3[:, 0, :, cols] = nn(spread, t_a).astype(BF).reshape(DEPTH, 8, STEP)
        s3[:, 1, :, cols] = nn(spread, t_b).astype(BF).reshape(DEPTH, 8, STEP)

    def third(k):
        zp = lax.rem(level + k, DEPTH)
        return remote(s3.at[zp], r3.at[k], send3.at[k], recv3.at[k], dp=zp)

    each(1, DEPTH, lambda k: third(k).start())

    each(1, PEERS, lambda k: return_rows(k).wait_recv())
    place = lax.broadcasted_iota(jnp.int32, (OWNED * HALF, 2 * HALF), 0)
    slot = lax.broadcasted_iota(jnp.int32, (OWNED * HALF, 2 * HALF), 1)
    pick = []
    for t in range(PEERS // 2):
        lo = (tab[2 * t, 0, me] - 1) * HALF
        hi = (tab[2 * t + 1, 0, me] - 1) * HALF
        target = jnp.where(slot < HALF, slot + lo, slot - HALF + hi)
        live = jnp.where(slot < HALF, lo, hi) >= 0
        pick.append(jnp.logical_and(place == target, live).astype(F32).astype(BF))
    total = nn(jnp.concatenate(pick, axis=1), recv[...].reshape(PEERS * HALF, D_ENC))
    ohalf[...] = total.astype(BF).reshape(OWNED, HALF, D_ENC)
    back = remote(ohalf, ge_hbm.at[:, mine], back_sem.at[0], back_sem.at[1], head=other)
    back.start()
    ge_out = pltpu.make_async_copy(ohalf, ge_hbm.at[:, mine], osem.at[1])
    ge_out.start()

    each(1, DEPTH, lambda k: third(k).wait())
    final = up(s3[level])
    for k in range(1, DEPTH):
        final = final + up(r3[k])
    gw_ref[:, 0, :] = final[0, :PIECE]
    gw_ref[:, 1, :] = final[1, :PIECE]

    each(1, PEERS, lambda k: ask(k).wait_send())
    each(1, PEERS, lambda k: share_rows(k).wait_send())
    each(1, PEERS, lambda k: return_rows(k).wait_send())
    gq_out.wait()
    ge_out.wait()
    back.wait()


def body(queries, out_grad, encodings, owner_map, nbr_count, key_weight, value_weight):
    vm = pl.BlockSpec(memory_space=pltpu.VMEM)
    sm = pl.BlockSpec(memory_space=pltpu.SMEM)
    hbm = pl.BlockSpec(memory_space=pl.ANY)
    dma = pltpu.SemaphoreType.DMA

    def bf(*shape):
        return pltpu.VMEM(shape, BF)

    gq, ge, gw = pl.pallas_call(
        kernel,
        out_shape=(
            jax.ShapeDtypeStruct((ROWS, FEAT), BF),
            jax.ShapeDtypeStruct((OWNED, NROWS, D_ENC), BF),
            jax.ShapeDtypeStruct((PIECE, 2, FEAT), F32),
        ),
        in_specs=[sm, sm, hbm, hbm, hbm, hbm, hbm],
        out_specs=(hbm, hbm, vm),
        scratch_shapes=[
            bf(OWNED, NROWS, D_ENC),
            bf(GROUPS, D_ENC, STEP),
            bf(GROUPS, D_ENC, STEP),
            bf(GROUPS, ROWS + RIM, STEP),
            bf(GROUPS, ROWS + RIM, STEP),
            pltpu.VMEM((1, 128), jnp.int32),
            pltpu.VMEM((PEERS, 1, 128), jnp.int32),
            pltpu.SMEM((PEERS, 1, 128), jnp.int32),
            bf(PEERS, HALF, D_ENC),
            bf(PEERS, NROWS, D_ENC),
            bf(PEERS, GROUPS, NROWS, STEP),
            bf(PEERS, GROUPS, NROWS, STEP),
            bf(PEERS, D_ENC, NROWS),
            bf(D_ENC, REFS * NROWS),
            bf(GROUPS, REFS * NROWS, STEP),
            bf(GROUPS, REFS * NROWS, STEP),
            pltpu.VMEM((REFS, NROWS, D_ENC), F32),
            pltpu.VMEM((REFS, HALF, D_ENC), F32),
            bf(REFS, HALF, D_ENC),
            bf(PEERS, HALF, D_ENC),
            bf(OWNED, HALF, D_ENC),
            bf(GROUPS, ROWS, STEP),
            bf(GROUPS, RIM, STEP),
            bf(ROWS, FEAT),
            bf(GROUPS, 2, SIDE, SIDE, SHARE, STEP),
            bf(GROUPS, SIDE - 1, SIDE, SHARE, STEP),
            bf(GROUPS, SIDE - 1, SIDE, SHARE, STEP),
            bf(GROUPS, SIDE, SHARE, STEP),
            bf(GROUPS, SIDE, SHARE, STEP),
            bf(GROUPS, SIDE - 1, SHARE, STEP),
            bf(GROUPS, SIDE - 1, SHARE, STEP),
            bf(DEPTH, 2, 8, FEAT),
            bf(DEPTH, 2, 8, FEAT),
            dma((18,)), dma((2,)),
            dma((PEERS,)), dma((PEERS,)), dma((PEERS,)), dma((PEERS,)), dma((PEERS,)), dma((PEERS,)),
            dma((2,)), dma((2,)), dma((2,)),
            dma((PEERS,)), dma((PEERS,)), dma((2,)), dma((2,)),
            dma((GROUPS, 3)), dma((GROUPS, 3)), dma((GROUPS, 3)), dma((GROUPS, 3)),
            dma((GROUPS, 3)), dma((GROUPS, 3)), dma((GROUPS, 3)), dma((GROUPS, 3)),
            dma((DEPTH,)), dma((DEPTH,)),
        ],
        compiler_params=pltpu.CompilerParams(
            collective_id=0, has_side_effects=True, vmem_limit_bytes=VMEM_LIMIT
        ),
        name="spans",
    )(
        owner_map[0], nbr_count, encodings.reshape(OWNED, NROWS, D_ENC),
        queries[0], out_grad[0], key_weight, value_weight,
    )
    return gq[None], ge.reshape(1, OWNED * NROWS, D_ENC), gw


def solution(mesh):
    return jax.shard_map(
        body,
        mesh=mesh,
        in_specs=(
            P("dp", "seq", "head"),
            P("dp", "seq", "head"),
            P("dp", "seq", None),
            P("dp", "seq", None),
            P("dp", "seq"),
            P(None, "head"),
            P(None, "head"),
        ),
        out_specs=(P("dp", "seq", "head"), P("dp", "seq", None), P(("seq", "dp"), None, "head")),
        check_vma=False,
    )
```

time: 627 us -> 121 us (0.19)
  waiting for transfers between devices: 307 us -> 0 us
  Pallas kernels: 0 us -> 113 us
  local copies, waits for them, and re-layouts: 94 us -> 6.71 us
  blocking collectives: 75.9 us -> 0 us
  matrix products: 72.2 us -> 0 us
  starting transfers between devices: 42 us -> 0 us
  between operations: 15.2 us -> 0.64 us
  other arithmetic: 13.9 us -> 0 us
    unnamed x2 -> x0, waiting for transfers between devices: 212 us -> none
    pallas_call x0 -> x1, Pallas kernels: none -> 113 us  [body(): pl.pallas_call(kernel, out_shape=(jax.ShapeDtypeStruct((ROWS, FEAT), BF),...]
    dot_general x14 -> x0, matrix products: 72.2 us -> none  [the longest x1 9.74 us: body(): jnp.einsum('rc,rf->cf', enc_columns, summed_keys, precision=highest)]
    all_to_all x1 -> x0, blocking collectives: 54.8 us -> none  [body(): lax.all_to_all(send_keys, 'seq', split_axis=0, concat_axis=0, tiled=True)]
    ppermute x3 -> x0, waiting for transfers between devices: 48.5 us -> none  [passed_along(): return lax.ppermute(shard, axis, pairs)]
    all_to_all x4 -> x0, waiting for transfers between devices: 46.2 us -> none  [the longest x1 23.9 us: body(): lax.all_to_all(blank_slots.at[slot_of].set(ref_value_grad), 'seq', split_...]
    all_to_all x4 -> x0, starting transfers between devices: 34.5 us -> none  [the longest x1 11.2 us: body(): lax.all_to_all(blank_slots.at[slot_of].set(ref_key_grad), 'seq', split_ax...]
    psum x1 -> x0, blocking collectives: 21.1 us -> none  [body(): grad_enc = lax.psum(enc_partial, 'head').astype(jnp.bfloat16)[None]]
  transfers between devices with their start and end apart: 8 -> 0, of which waited for: 5 -> 0; matrix products, arithmetic and copies ran while one was open for 14% -> 0% of each run, Pallas kernels for 0% -> 0%
where the time goes in v2:
time: 121 us; the launch traced here: 120 us
  Pallas kernels  113 us (93%)
  local copies, waits for them, and re-layouts  6.71 us (6%)
    pallas_call x1, Pallas kernels, body(): pl.pallas_call(kernel, out_shape=(jax.ShapeDtypeStruct((ROWS, FEAT), BF),...  113 us
    unnamed x5, local copies, waits for them, and re-layouts  5.37 us

profile of v2, /device:TPU:1, one launch (start us, length us, event | category | flops | bytes accessed | tf_op | source)
XLA Modules:
  0.0 120.2 jit_solution(10550855281296467154)
XLA Ops:
  0.6 1.3 %copy.10.map_ref = s32[4,2]{1,0:T(4,128)} copy(s32[4,2]{0,1:T(2,128)} %bitcast.11) | data formatting | bytes 64 | tf_op jit(solution)/shard_map/squeeze | solution.py:443
  2.0 112.9 %spans.1 = (bf16[256,1024]{1,0:T(8,128)(2,1)}, bf16[8,128,896]{2,1,0:T(8,128)(2,1)}, f32[7,2,1024]{2,1,0:T(2,128)}) custom-call(s32[4,2]{1,0:T(4,128)} %copy.10.map_ref, s32[1,4]{1,0:T(1,128)} %cnt_ref.1, bf16[8,128,896]{2,1,0:T(8,128)(2,1)} %bitcast.7, bf16[256,1024]{1,0:T(8,128)(2,1)} %bitcast.8, bf16[256,1024]{1,0:T(8,128)(2,1)} %bitcast.9, ...), custom_call_target="tpu_custom_call" | custom-call | tf_op jit(solution)/shard_map/spans/pallas_call | solution.py:387
  114.9 1.9 %copy.14 = bf16[1,256,1024]{2,1,0:T(8,128)(2,1)} copy(bf16[1,256,1024]{2,1,0:T(8,128)(2,1)} %bitcast.10) | data formatting | bytes 1048576
  116.7 0.0 copy-start
  116.7 2.9 %copy.15 = bf16[1,1024,896]{2,1,0:T(8,128)(2,1)} copy(bf16[1,1024,896]{2,1,0:T(8,128)(2,1)} %bitcast.6) | data formatting | bytes 3670016
  119.6 0.0 copy-done
  119.6 0.6 copy.16
Async XLA Ops:
  116.7 2.9 %copy-start = (f32[7,2,1024]{2,1,0:T(2,128)S(1)}, f32[7,2,1024]{2,1,0:T(2,128)}, u32[]{:S(2)}) copy-start(f32[7,2,1024]{2,1,0:T(2,128)} %get-tuple-element.14) | copy-start | bytes 172036

commit v3 on v2

v3 whole, which is shorter than its diff:
```python
import functools
import math

import jax
import jax.numpy as jnp
from jax import lax
from jax.experimental import pallas as pl
from jax.experimental.pallas import tpu as pltpu
from jax.sharding import PartitionSpec as P

MESH = pl.DeviceIdType.MESH
HD = 128
SPAN = 64
NROWS = 128
REFS = 8
SIDE = 4
PEERS = SIDE * SIDE
DEPTH = 8
HALF = NROWS // 2
OWNED = 8
D_ENC = 896
FEAT = 1024
ROWS = 256
RIM = 64
STEP = 256
GROUPS = FEAT // STEP
SHARE = D_ENC // PEERS
PIECE = SHARE // DEPTH
VMEM_LIMIT = 58 << 20
BF = jnp.bfloat16
F32 = jnp.float32


def ring(step):
    return min(step, SIDE - step)


STEPS = sorted(
    [(dx, dy) for dx in range(SIDE) for dy in range(SIDE)],
    key=lambda s: -(ring(s[0]) + ring(s[1])) if s != (0, 0) else -9,
)


def plane_place():
    me = lax.axis_index("seq")
    return me, lax.div(me, SIDE), lax.rem(me, SIDE)


def plane_peer(x, y, i):
    dx, dy = STEPS[i]
    return lax.rem(x + dx, SIDE) * SIDE + lax.rem(y + dy, SIDE)


def opposite(i):
    dx, dy = STEPS[i]
    return STEPS.index((-dx % SIDE, -dy % SIDE))


def each(start, stop, step):
    def one(k, carry):
        step(k)
        return carry

    lax.fori_loop(start, stop, one, 0)


def up(a):
    return a.astype(F32)


def remote(src, dst, send_sem, recv_sem, **where):
    return pltpu.make_async_remote_copy(
        src_ref=src,
        dst_ref=dst,
        send_sem=send_sem,
        recv_sem=recv_sem,
        device_id=where,
        device_id_type=MESH,
    )


def greet(barrier, **where):
    pl.semaphore_signal(barrier, inc=1, device_id=where, device_id_type=MESH)


def nt(a, b):
    return lax.dot_general(a, b, (((1,), (1,)), ((), ())), preferred_element_type=F32)


def tn(a, b):
    return lax.dot_general(a, b, (((0,), (0,)), ((), ())), preferred_element_type=F32)


def nn(a, b):
    return jnp.dot(a, b, preferred_element_type=F32)


def shift_matrix(rows, columns, by):
    i = lax.broadcasted_iota(jnp.int32, (rows, columns), 0)
    e = lax.broadcasted_iota(jnp.int32, (rows, columns), 1)
    return (e == i + by).astype(F32).astype(BF)


def kernel(
    map_ref, cnt_ref, enc_hbm, q_hbm, d_hbm, wk_hbm, wv_hbm,
    gq_hbm, ge_hbm, gw_ref,
    enc, w, qx, dx, asked, tabv, tab, send, slots, kv, enct, refs_t,
    dkv, con, hbuf, half, recv, ohalf, gs, prev, gqv, dw, r1a, r1b, s2a, s2b, r2a, r2b, s3, r3,
    lsem, osem, isend, irecv, ssend, srecv, fsend, frecv, halo_send, halo_recv,
    swap_sem, rsend, rrecv, back_sem, prev_sem,
    send1a, recv1a, send1b, recv1b, send2a, recv2a, send2b, recv2b, send3, recv3,
):
    me, x, y = plane_place()
    core = lax.axis_index("head")
    level = lax.axis_index("dp")
    other = 1 - core
    scale = 1.0 / math.sqrt(HD)
    mine = pl.ds(pl.multiple_of(core * HALF, HALF), HALF)
    theirs = pl.ds(pl.multiple_of(other * HALF, HALF), HALF)
    before = lax.rem(me + PEERS - 1, PEERS)
    after = lax.rem(me + 1, PEERS)

    barrier = pltpu.get_barrier_semaphore()
    for i in range(1, PEERS):
        greet(barrier, seq=plane_peer(x, y, i))
    greet(barrier, head=other)
    each(1, DEPTH, lambda k: greet(barrier, dp=lax.rem(level + k, DEPTH)))

    enc_load = pltpu.make_async_copy(enc_hbm, enc, lsem.at[0])
    loads = [
        pltpu.make_async_copy(q_hbm, qx.at[pl.ds(0, ROWS)], lsem.at[1]),
        pltpu.make_async_copy(d_hbm, dx.at[pl.ds(0, ROWS)], lsem.at[2]),
    ]
    weights = [
        pltpu.make_async_copy(wk_hbm, w.at[:, pl.ds(0, FEAT)], lsem.at[3]),
        pltpu.make_async_copy(wv_hbm, w.at[:, pl.ds(FEAT, FEAT)], lsem.at[4]),
    ]
    for c in [enc_load] + weights + loads:
        c.start()

    lane = lax.broadcasted_iota(jnp.int32, (1, 128), 1)
    row = jnp.zeros((1, 128), jnp.int32)
    owners, kin = [], []
    for r in range(REFS):
        entry = map_ref[0, r // 2, r % 2]
        owner = lax.div(entry, OWNED)
        row = jnp.where(lane == owner, lax.rem(entry, OWNED) + 1, row)
        owners.append(owner)
        kx = lax.rem(x - lax.div(owner, SIDE) + SIDE, SIDE)
        ky = lax.rem(y - lax.rem(owner, SIDE) + SIDE, SIDE)
        found = jnp.int32(0)
        for i in range(1, PEERS):
            found = jnp.where(kx * SIDE + ky == STEPS[i][0] * SIDE + STEPS[i][1], jnp.int32(i), found)
        kin.append(found)
    asked[...] = row
    tabv[0] = row
    pl.semaphore_wait(barrier, PEERS + DEPTH - 1)

    def ask(i, peer):
        return remote(asked, tabv.at[i], isend.at[i], irecv.at[i], seq=peer)

    for i in range(1, PEERS):
        ask(i, plane_peer(x, y, i)).start()
    halos = [
        remote(q_hbm.at[pl.ds(0, RIM)], qx.at[pl.ds(ROWS, RIM)], halo_send.at[0], halo_recv.at[0], seq=before),
        remote(d_hbm.at[pl.ds(0, RIM)], dx.at[pl.ds(ROWS, RIM)], halo_send.at[1], halo_recv.at[1], seq=before),
    ]
    for c in halos:
        c.start()
    each(1, PEERS, lambda i: ask(i, after).wait_recv())
    lc = pltpu.make_async_copy(tabv, tab, lsem.at[5])
    lc.start()
    enc_load.wait()
    lc.wait()

    def give_rows(i, peer):
        return remote(send.at[i], slots.at[i, mine], ssend.at[i], srecv.at[i], seq=peer)

    def share_rows(i):
        part = slots.at[i, mine]
        return remote(part, part, fsend.at[i], frecv.at[i], head=other)

    for i in range(1, PEERS):
        place = jnp.maximum(tab[opposite(i), 0, me] - 1, 0)
        send[i] = enc[place, mine, :]
        give_rows(i, plane_peer(x, y, i)).start()
    slots[0] = enc[jnp.maximum(tab[0, 0, me] - 1, 0)]
    for c in weights:
        c.wait()

    def project(j):
        block = slots[pl.ds(2 * j, 2)].reshape(2 * NROWS, D_ENC)
        for g in range(2 * GROUPS):
            cols = pl.ds(g * STEP, STEP)
            kv[pl.ds(2 * j, 2), :, cols] = nn(block, w[:, cols]).astype(BF).reshape(2, NROWS, STEP)
        enct[2 * j] = block[:NROWS].T
        enct[2 * j + 1] = block[NROWS:].T

    def arrive(i):
        give_rows(i, after).wait_recv()
        share_rows(i).start()

    arrive(1)

    def pair(j):
        @pl.when(j < PEERS // 2 - 1)
        def _():
            arrive(2 * j + 2)
            arrive(2 * j + 3)

        @pl.when(j > 0)
        def _():
            share_rows(2 * j).wait_recv()

        share_rows(2 * j + 1).wait_recv()
        project(j)

    each(0, PEERS // 2, pair)
    for c in loads:
        c.wait()
    for c in halos:
        c.wait()
    for r in range(REFS):
        refs_t[:, pl.ds(r * NROWS, NROWS)] = enct[kin[r]]

    move = shift_matrix(ROWS, ROWS + RIM, RIM - 1)
    inside = lax.broadcasted_iota(jnp.int32, (ROWS, ROWS + RIM), 1) < jnp.where(me == PEERS - 1, ROWS, ROWS + RIM)
    move = jnp.where(inside, up(move), 0.0).astype(BF)
    col = lax.broadcasted_iota(jnp.int32, (SPAN, 2 * NROWS), 1)

    def first_a(g, k):
        xp = lax.rem(x + k, SIDE)
        return remote(dw.at[g, 0, xp], r1a.at[g, k - 1], send1a.at[g, k - 1], recv1a.at[g, k - 1], seq=xp * SIDE + y)

    def first_b(g, k):
        yp = lax.rem(y + k, SIDE)
        return remote(dw.at[g, 1, :, yp], r1b.at[g, k - 1], send1b.at[g, k - 1], recv1b.at[g, k - 1], seq=x * SIDE + yp)

    def second_a(p, k):
        yp = lax.rem(y + k, SIDE)
        return remote(s2a.at[p, :, yp], r2a.at[p, k - 1], send2a.at[p, k - 1], recv2a.at[p, k - 1], seq=x * SIDE + yp)

    def second_b(p, k):
        xp = lax.rem(x + k, SIDE)
        return remote(s2b.at[p, :, xp], r2b.at[p, k - 1], send2b.at[p, k - 1], recv2b.at[p, k - 1], seq=xp * SIDE + y)

    def sum_first(g):
        for k in (1, 2, 3):
            first_a(g, k).wait()
            first_b(g, k).wait()
        p, n = lax.div(g, 2), lax.rem(g, 2)
        for j in range(SIDE):
            s2a[p, n, j] = (up(dw[g, 0, x, j]) + up(r1a[g, 0, j]) + up(r1a[g, 1, j]) + up(r1a[g, 2, j])).astype(BF)
            s2b[p, n, j] = (up(dw[g, 1, j, y]) + up(r1b[g, 0, j]) + up(r1b[g, 1, j]) + up(r1b[g, 2, j])).astype(BF)

    def start_second(p):
        for k in (2, 1, 3):
            second_a(p, k).start()
            second_b(p, k).start()

    def group(g):
        cols = pl.ds(pl.multiple_of(g * STEP, STEP), STEP)
        cols_v = pl.ds(pl.multiple_of(g * STEP + FEAT, STEP), STEP)
        qs = nn(move, qx[:, cols]).astype(BF)
        do = nn(move, dx[:, cols]).astype(BF)
        units = [(c, h) for c in range(REFS // 2) for h in range(STEP // HD)]

        def cut(a, c, h):
            return a[c * SPAN : (c + 1) * SPAN, h * HD : (h + 1) * HD]

        def head(h, base=0):
            return pl.ds(pl.multiple_of(g * STEP + h * HD + base, HD), HD)

        def both(c, h, base):
            return jnp.concatenate([kv[kin[2 * c + n], :, head(h, base)] for n in range(2)], axis=0)

        k_u = [both(c, h, 0) for c, h in units]
        v_u = [both(c, h, FEAT) for c, h in units]
        q_u = [cut(qs, c, h) for c, h in units]
        d_u = [cut(do, c, h) for c, h in units]
        scores = [nt(q, k) * scale for q, k in zip(q_u, k_u)]
        dprobs = [nt(d, v) for d, v in zip(d_u, v_u)]
        probs_b, ds_b = [], []
        for (c, h), s, dp in zip(units, scores, dprobs):
            s = jnp.where(col < cnt_ref[0, c] * NROWS, s, -1e30)
            e = jnp.exp(s - jnp.max(s, axis=-1, keepdims=True))
            p = e / jnp.sum(e, axis=-1, keepdims=True)
            pb = p.astype(BF)
            delta = jnp.sum(up(pb) * dp, axis=-1, keepdims=True)
            probs_b.append(pb)
            ds_b.append((p * (dp - delta)).astype(BF))
        for (c, h), q, d, k, pb, ds in zip(units, q_u, d_u, k_u, probs_b, ds_b):
            two = pl.ds(2 * c, 2)
            gs[pl.ds(c * SPAN, SPAN), head(h)] = (nn(ds, k) * scale).astype(BF)
            dkv[two, :, head(h)] = (tn(ds, q) * scale).astype(BF).reshape(2, NROWS, HD)
            dkv[two, :, head(h, FEAT)] = tn(pb, d).astype(BF).reshape(2, NROWS, HD)
        dk = dkv[:, :, cols].reshape(REFS * NROWS, STEP)
        dv = dkv[:, :, cols_v].reshape(REFS * NROWS, STEP)
        dw[g, 0] = nn(refs_t[...], dk).astype(BF).reshape(SIDE, SIDE, SHARE, STEP)
        dw[g, 1] = nn(refs_t[...], dv).astype(BF).reshape(SIDE, SIDE, SHARE, STEP)
        for k in (2, 1, 3):
            first_a(g, k).start()
            first_b(g, k).start()

        @pl.when(g >= 2)
        def _():
            sum_first(g - 2)

    each(0, GROUPS, group)
    start_second(0)

    con[...] = nt(dkv[:, theirs, :].reshape(REFS * HALF, 2 * FEAT), w[...]).reshape(REFS, HALF, D_ENC)
    swap = remote(con, hbuf, swap_sem.at[0], swap_sem.at[1], head=other)
    swap.start()
    own = nt(dkv[:, mine, :].reshape(REFS * HALF, 2 * FEAT), w[...]).reshape(REFS, HALF, D_ENC)
    swap.wait()
    half[...] = (own + hbuf[...]).astype(BF)

    def ref_for(peer):
        found = jnp.int32(0)
        for r in range(REFS):
            found = jnp.where(owners[r] == peer, jnp.int32(r), found)
        return found

    each(1, PEERS, lambda i: give_rows(i, after).wait_send())

    def return_rows(i, peer):
        return remote(send.at[i], recv.at[i], rsend.at[i], rrecv.at[i], seq=peer)

    for i in range(1, PEERS):
        peer = plane_peer(x, y, i)
        send[i] = half[ref_for(peer)]
        return_rows(i, peer).start()
    halo = remote(gs.at[pl.ds(ROWS - RIM, RIM)], prev, prev_sem.at[0], prev_sem.at[1], seq=after)
    halo.start()
    recv[0] = half[ref_for(me)]
    sum_first(2)
    sum_first(3)
    start_second(1)

    halo.wait()
    old = jnp.where(me == 0, 0.0, 1.0)
    ext = jnp.concatenate([(up(prev[...]) * old).astype(BF), gs[...]], axis=0)
    gqv[...] = nn(shift_matrix(ROWS, ROWS + RIM, 1), ext).astype(BF)
    gq_out = pltpu.make_async_copy(gqv, gq_hbm, osem.at[0])
    gq_out.start()

    m = lax.broadcasted_iota(jnp.int32, (DEPTH * 8, SHARE), 0)
    e = lax.broadcasted_iota(jnp.int32, (DEPTH * 8, SHARE), 1)
    spread = jnp.logical_and(m // 8 * PIECE + m % 8 == e, m % 8 < PIECE).astype(F32).astype(BF)
    for p in range(GROUPS // 2):
        for k in (1, 2, 3):
            second_a(p, k).wait()
            second_b(p, k).wait()
        for n in range(2):
            g = 2 * p + n
            own_a = up(dw[g, 0, x, y]) + up(r1a[g, 0, y]) + up(r1a[g, 1, y]) + up(r1a[g, 2, y])
            own_b = up(dw[g, 1, x, y]) + up(r1b[g, 0, x]) + up(r1b[g, 1, x]) + up(r1b[g, 2, x])
            t_a = (own_a + up(r2a[p, 0, n]) + up(r2a[p, 1, n]) + up(r2a[p, 2, n])).astype(BF)
            t_b = (own_b + up(r2b[p, 0, n]) + up(r2b[p, 1, n]) + up(r2b[p, 2, n])).astype(BF)
            cols = pl.ds(g * STEP, STEP)
            s3[:, 0, :, cols] = nn(spread, t_a).astype(BF).reshape(DEPTH, 8, STEP)
            s3[:, 1, :, cols] = nn(spread, t_b).astype(BF).reshape(DEPTH, 8, STEP)

    def third(k):
        zp = lax.rem(level + k, DEPTH)
        return remote(s3.at[zp], r3.at[k], send3.at[k], recv3.at[k], dp=zp)

    for k in (4, 3, 5, 2, 6, 1, 7):
        third(k).start()

    place = lax.broadcasted_iota(jnp.int32, (OWNED * HALF, 2 * HALF), 0)
    slot = lax.broadcasted_iota(jnp.int32, (OWNED * HALF, 2 * HALF), 1)
    pick = []
    for t in range(PEERS // 2):
        lo = (tab[2 * t, 0, me] - 1) * HALF
        hi = (tab[2 * t + 1, 0, me] - 1) * HALF
        target = jnp.where(slot < HALF, slot + lo, slot - HALF + hi)
        live = jnp.where(slot < HALF, lo, hi) >= 0
        pick.append(jnp.logical_and(place == target, live).astype(F32).astype(BF))
    pick = jnp.concatenate(pick, axis=1)
    each(1, PEERS, lambda i: return_rows(i, after).wait_recv())
    total = nn(pick, recv[...].reshape(PEERS * HALF, D_ENC))
    ohalf[...] = total.astype(BF).reshape(OWNED, HALF, D_ENC)
    back = remote(ohalf, ge_hbm.at[:, mine], back_sem.at[0], back_sem.at[1], head=other)
    back.start()
    ge_out = pltpu.make_async_copy(ohalf, ge_hbm.at[:, mine], osem.at[1])
    ge_out.start()

    each(1, DEPTH, lambda k: third(k).wait())
    final = up(s3[level])
    for k in range(1, DEPTH):
        final = final + up(r3[k])
    gw_ref[:, 0, :] = final[0, :PIECE]
    gw_ref[:, 1, :] = final[1, :PIECE]

    each(1, PEERS, lambda i: ask(i, after).wait_send())
    each(1, PEERS, lambda i: share_rows(i).wait_send())
    each(1, PEERS, lambda i: return_rows(i, after).wait_send())
    gq_out.wait()
    ge_out.wait()
    back.wait()


def finish_kernel(gq, ge, gw, gq_out, ge_out, gw_out, sems):
    copies = [pltpu.make_async_copy(gw, gw_out, sems.at[0])]
    for n in range(4):
        two = pl.ds(2 * n, 2)
        copies.append(pltpu.make_async_copy(ge.at[two], ge_out.at[two], sems.at[1 + n]))
    for n in range(2):
        rows = pl.ds(n * ROWS // 2, ROWS // 2)
        copies.append(pltpu.make_async_copy(gq.at[rows], gq_out.at[rows], sems.at[5 + n]))
    for c in copies:
        c.start()
    for c in copies:
        c.wait()


def body(queries, out_grad, encodings, owner_map, nbr_count, key_weight, value_weight):
    vm = pl.BlockSpec(memory_space=pltpu.VMEM)
    sm = pl.BlockSpec(memory_space=pltpu.SMEM)
    hbm = pl.BlockSpec(memory_space=pl.ANY)
    dma = pltpu.SemaphoreType.DMA

    def bf(*shape):
        return pltpu.VMEM(shape, BF)

    gq, ge, gw = pl.pallas_call(
        kernel,
        out_shape=(
            jax.ShapeDtypeStruct((ROWS, FEAT), BF),
            jax.ShapeDtypeStruct((OWNED, NROWS, D_ENC), BF),
            jax.ShapeDtypeStruct((PIECE, 2, FEAT), F32),
        ),
        in_specs=[sm, sm, hbm, hbm, hbm, hbm, hbm],
        out_specs=(hbm, hbm, vm),
        scratch_shapes=[
            bf(OWNED, NROWS, D_ENC),
            bf(D_ENC, 2 * FEAT),
            bf(ROWS + RIM, FEAT),
            bf(ROWS + RIM, FEAT),
            pltpu.VMEM((1, 128), jnp.int32),
            pltpu.VMEM((PEERS, 1, 128), jnp.int32),
            pltpu.SMEM((PEERS, 1, 128), jnp.int32),
            bf(PEERS, HALF, D_ENC),
            bf(PEERS, NROWS, D_ENC),
            bf(PEERS, NROWS, 2 * FEAT),
            bf(PEERS, D_ENC, NROWS),
            bf(D_ENC, REFS * NROWS),
            bf(REFS, NROWS, 2 * FEAT),
            pltpu.VMEM((REFS, HALF, D_ENC), F32),
            pltpu.VMEM((REFS, HALF, D_ENC), F32),
            bf(REFS, HALF, D_ENC),
            bf(PEERS, HALF, D_ENC),
            bf(OWNED, HALF, D_ENC),
            bf(ROWS, FEAT),
            bf(RIM, FEAT),
            bf(ROWS, FEAT),
            bf(GROUPS, 2, SIDE, SIDE, SHARE, STEP),
            bf(GROUPS, SIDE - 1, SIDE, SHARE, STEP),
            bf(GROUPS, SIDE - 1, SIDE, SHARE, STEP),
            bf(GROUPS // 2, 2, SIDE, SHARE, STEP),
            bf(GROUPS // 2, 2, SIDE, SHARE, STEP),
            bf(GROUPS // 2, SIDE - 1, 2, SHARE, STEP),
            bf(GROUPS // 2, SIDE - 1, 2, SHARE, STEP),
            bf(DEPTH, 2, 8, FEAT),
            bf(DEPTH, 2, 8, FEAT),
            dma((6,)), dma((2,)),
            dma((PEERS,)), dma((PEERS,)), dma((PEERS,)), dma((PEERS,)), dma((PEERS,)), dma((PEERS,)),
            dma((2,)), dma((2,)), dma((2,)),
            dma((PEERS,)), dma((PEERS,)), dma((2,)), dma((2,)),
            dma((GROUPS, 3)), dma((GROUPS, 3)), dma((GROUPS, 3)), dma((GROUPS, 3)),
            dma((2, 3)), dma((2, 3)), dma((2, 3)), dma((2, 3)),
            dma((DEPTH,)), dma((DEPTH,)),
        ],
        compiler_params=pltpu.CompilerParams(
            collective_id=0, has_side_effects=True, vmem_limit_bytes=VMEM_LIMIT
        ),
        name="spans",
    )(
        owner_map, nbr_count, encodings.reshape(OWNED, NROWS, D_ENC),
        queries[0], out_grad[0], key_weight, value_weight,
    )
    gq, ge, gw = pl.pallas_call(
        finish_kernel,
        out_shape=tuple(jax.ShapeDtypeStruct(a.shape, a.dtype) for a in (gq, ge, gw)),
        in_specs=[hbm] * 3,
        out_specs=(hbm,) * 3,
        scratch_shapes=[dma((7,))],
        name="finish",
    )(gq, ge, gw)
    return gq[None], ge.reshape(1, OWNED * NROWS, D_ENC), gw


def solution(mesh):
    return jax.shard_map(
        body,
        mesh=mesh,
        in_specs=(
            P("dp", "seq", "head"),
            P("dp", "seq", "head"),
            P("dp", "seq", None),
            P("dp", "seq", None),
            P("dp", "seq"),
            P(None, "head"),
            P(None, "head"),
        ),
        out_specs=(P("dp", "seq", "head"), P("dp", "seq", None), P(("seq", "dp"), None, "head")),
        check_vma=False,
    )
```

time: 121 us -> 187 us (1.55)
  Pallas kernels: 113 us -> 185 us
  local copies, waits for them, and re-layouts: 6.71 us -> 1.34 us
    pallas_call x0 -> x1, Pallas kernels: none -> 74.4 us  [body(): pl.pallas_call(finish_kernel, out_shape=tuple((jax.ShapeDtypeStruct(a.sha...]
    unnamed x5 -> x1, local copies, waits for them, and re-layouts: 5.37 us -> 1.34 us
    pallas_call x1, Pallas kernels: 113 us -> 110 us  [body(): pl.pallas_call(kernel, out_shape=(jax.ShapeDtypeStruct((ROWS, FEAT), BF),...]
where the time goes in v3:
time: 187 us
  Pallas kernels  185 us (99%)
    pallas_call x1, Pallas kernels, body(): pl.pallas_call(kernel, out_shape=(jax.ShapeDtypeStruct((ROWS, FEAT), BF),...  110 us
    pallas_call x1, Pallas kernels, body(): pl.pallas_call(finish_kernel, out_shape=tuple((jax.ShapeDtypeStruct(a.sha...  74.4 us

profile of v3, /device:TPU:1, one launch (start us, length us, event | category | flops | bytes accessed | tf_op | source)
XLA Modules:
  0.0 186.5 jit_solution(737442124333445238)
XLA Ops:
  0.6 1.3 copy.10.map_ref
  2.0 110.2 %spans.1 = (bf16[256,1024]{1,0:T(8,128)(2,1)}, bf16[8,128,896]{2,1,0:T(8,128)(2,1)}, f32[7,2,1024]{2,1,0:T(2,128)}) custom-call(s32[1,4,2]{2,1,0:T(4,128)} %copy.10.map_ref, s32[1,4]{1,0:T(1,128)} %cnt_ref.1, bf16[8,128,896]{2,1,0:T(8,128)(2,1)} %bitcast.5, bf16[256,1024]{1,0:T(8,128)(2,1)} %bitcast.6, bf16[256,1024]{1,0:T(8,128)(2,1)} %bitcast.7, ...), custom_call_target="tpu_custom_call" | custom-call | tf_op jit(solution)/shard_map/spans/pallas_call | solution.py:428
  112.1 74.4 %finish.1 = (bf16[256,1024]{1,0:T(8,128)(2,1)}, bf16[8,128,896]{2,1,0:T(8,128)(2,1)}, f32[7,2,1024]{2,1,0:T(2,128)}) custom-call(bf16[256,1024]{1,0:T(8,128)(2,1)} %get-tuple-element.9.gq, bf16[8,128,896]{2,1,0:T(8,128)(2,1)} %get-tuple-element.10.ge, f32[7,2,1024]{2,1,0:T(2,128)} %get-tuple-element.11.gw), custom_call_target="tpu_custom_call" | custom-call | tf_op jit(solution)/shard_map/finish/pallas_call | solution.py:484

commit v4 on v3

--- a/solution.py
+++ b/solution.py
@@ -105,10 +105,10 @@
     map_ref, cnt_ref, enc_hbm, q_hbm, d_hbm, wk_hbm, wv_hbm,
     gq_hbm, ge_hbm, gw_ref,
     enc, w, qx, dx, asked, tabv, tab, send, slots, kv, enct, refs_t,
-    dkv, con, hbuf, half, recv, ohalf, gs, prev, gqv, dw, r1a, r1b, s2a, s2b, r2a, r2b, s3, r3,
+    dkv, con, hbuf, half, recv, ohalf, gs, prev, gqv, dw, r1a, r1b, s2a, s2b, r2a, r2b, s3, r3, zs, zr, zt, zu,
     lsem, osem, isend, irecv, ssend, srecv, fsend, frecv, halo_send, halo_recv,
     swap_sem, rsend, rrecv, back_sem, prev_sem,
-    send1a, recv1a, send1b, recv1b, send2a, recv2a, send2b, recv2b, send3, recv3,
+    send1a, recv1a, send1b, recv1b, send2a, recv2a, send2b, recv2b, send3, recv3, zsend, zrecv, tsend, trecv,
 ):
     me, x, y = plane_place()
     core = lax.axis_index("head")
@@ -142,7 +142,7 @@
     row = jnp.zeros((1, 128), jnp.int32)
     owners, kin = [], []
     for r in range(REFS):
-        entry = map_ref[0, r // 2, r % 2]
+        entry = map_ref[0, r % 2, r // 2]
         owner = lax.div(entry, OWNED)
         row = jnp.where(lane == owner, lax.rem(entry, OWNED) + 1, row)
         owners.append(owner)
@@ -236,29 +236,31 @@
         yp = lax.rem(y + k, SIDE)
         return remote(dw.at[g, 1, :, yp], r1b.at[g, k - 1], send1b.at[g, k - 1], recv1b.at[g, k - 1], seq=x * SIDE + yp)
 
-    def second_a(p, k):
+    def second_a(k):
         yp = lax.rem(y + k, SIDE)
-        return remote(s2a.at[p, :, yp], r2a.at[p, k - 1], send2a.at[p, k - 1], recv2a.at[p, k - 1], seq=x * SIDE + yp)
-
-    def second_b(p, k):
+        return remote(s2a.at[:, yp], r2a.at[k - 1], send2a.at[k - 1], recv2a.at[k - 1], seq=x * SIDE + yp)
+
+    def second_b(k):
         xp = lax.rem(x + k, SIDE)
-        return remote(s2b.at[p, :, xp], r2b.at[p, k - 1], send2b.at[p, k - 1], recv2b.at[p, k - 1], seq=xp * SIDE + y)
+        return remote(s2b.at[:, xp], r2b.at[k - 1], send2b.at[k - 1], recv2b.at[k - 1], seq=xp * SIDE + y)
 
     def sum_first(g):
         for k in (1, 2, 3):
             first_a(g, k).wait()
             first_b(g, k).wait()
-        p, n = lax.div(g, 2), lax.rem(g, 2)
         for j in range(SIDE):
-            s2a[p, n, j] = (up(dw[g, 0, x, j]) + up(r1a[g, 0, j]) + up(r1a[g, 1, j]) + up(r1a[g, 2, j])).astype(BF)
-            s2b[p, n, j] = (up(dw[g, 1, j, y]) + up(r1b[g, 0, j]) + up(r1b[g, 1, j]) + up(r1b[g, 2, j])).astype(BF)
-
-    def start_second(p):
-        for k in (2, 1, 3):
-            second_a(p, k).start()
-            second_b(p, k).start()
-
-    def group(g):
+            s2a[g - 1, j] = (up(dw[g, 0, x, j]) + up(r1a[g, 0, j]) + up(r1a[g, 1, j]) + up(r1a[g, 2, j])).astype(BF)
+            s2b[g - 1, j] = (up(dw[g, 1, j, y]) + up(r1b[g, 0, j]) + up(r1b[g, 1, j]) + up(r1b[g, 2, j])).astype(BF)
+
+    m = lax.broadcasted_iota(jnp.int32, (DEPTH * 8, SHARE), 0)
+    e = lax.broadcasted_iota(jnp.int32, (DEPTH * 8, SHARE), 1)
+    spread = jnp.logical_and(m // 8 * PIECE + m % 8 == e, m % 8 < PIECE).astype(F32).astype(BF)
+
+    def level_first(k):
+        zp = lax.rem(level + k, DEPTH)
+        return remote(zs.at[zp], zr.at[k], zsend.at[k], zrecv.at[k], dp=zp)
+
+    def group(g, first=False):
         cols = pl.ds(pl.multiple_of(g * STEP, STEP), STEP)
         cols_v = pl.ds(pl.multiple_of(g * STEP + FEAT, STEP), STEP)
         qs = nn(move, qx[:, cols]).astype(BF)
@@ -298,16 +300,21 @@
         dv = dkv[:, :, cols_v].reshape(REFS * NROWS, STEP)
         dw[g, 0] = nn(refs_t[...], dk).astype(BF).reshape(SIDE, SIDE, SHARE, STEP)
         dw[g, 1] = nn(refs_t[...], dv).astype(BF).reshape(SIDE, SIDE, SHARE, STEP)
-        for k in (2, 1, 3):
-            first_a(g, k).start()
-            first_b(g, k).start()
-
-        @pl.when(g >= 2)
-        def _():
-            sum_first(g - 2)
-
-    each(0, GROUPS, group)
-    start_second(0)
+        if first:
+            for n in range(2):
+                for i in range(PEERS):
+                    zs[:, n, i] = nn(spread, dw[0, n, i // SIDE, i % SIDE]).astype(BF).reshape(DEPTH, 8, STEP)
+            for k in (4, 3, 5, 2, 6, 1, 7):
+                level_first(k).start()
+        else:
+            for k in (2, 1, 3):
+                first_a(g, k).start()
+                first_b(g, k).start()
+
+    group(0, first=True)
+    each(1, GROUPS, group)
+    halo = remote(gs.at[pl.ds(ROWS - RIM, RIM)], prev, prev_sem.at[0], prev_sem.at[1], seq=after)
+    halo.start()
 
     con[...] = nt(dkv[:, theirs, :].reshape(REFS * HALF, 2 * FEAT), w[...]).reshape(REFS, HALF, D_ENC)
     swap = remote(con, hbuf, swap_sem.at[0], swap_sem.at[1], head=other)
@@ -315,6 +322,10 @@
     own = nt(dkv[:, mine, :].reshape(REFS * HALF, 2 * FEAT), w[...]).reshape(REFS, HALF, D_ENC)
     swap.wait()
     half[...] = (own + hbuf[...]).astype(BF)
+    each(1, GROUPS, sum_first)
+    for k in (2, 1, 3):
+        second_a(k).start()
+        second_b(k).start()
 
     def ref_for(peer):
         found = jnp.int32(0)
@@ -331,12 +342,7 @@
         peer = plane_peer(x, y, i)
         send[i] = half[ref_for(peer)]
         return_rows(i, peer).start()
-    halo = remote(gs.at[pl.ds(ROWS - RIM, RIM)], prev, prev_sem.at[0], prev_sem.at[1], seq=after)
-    halo.start()
     recv[0] = half[ref_for(me)]
-    sum_first(2)
-    sum_first(3)
-    start_second(1)
 
     halo.wait()
     old = jnp.where(me == 0, 0.0, 1.0)
@@ -345,22 +351,17 @@
     gq_out = pltpu.make_async_copy(gqv, gq_hbm, osem.at[0])
     gq_out.start()
 
-    m = lax.broadcasted_iota(jnp.int32, (DEPTH * 8, SHARE), 0)
-    e = lax.broadcasted_iota(jnp.int32, (DEPTH * 8, SHARE), 1)
-    spread = jnp.logical_and(m // 8 * PIECE + m % 8 == e, m % 8 < PIECE).astype(F32).astype(BF)
-    for p in range(GROUPS // 2):
-        for k in (1, 2, 3):
-            second_a(p, k).wait()
-            second_b(p, k).wait()
-        for n in range(2):
-            g = 2 * p + n
-            own_a = up(dw[g, 0, x, y]) + up(r1a[g, 0, y]) + up(r1a[g, 1, y]) + up(r1a[g, 2, y])
-            own_b = up(dw[g, 1, x, y]) + up(r1b[g, 0, x]) + up(r1b[g, 1, x]) + up(r1b[g, 2, x])
-            t_a = (own_a + up(r2a[p, 0, n]) + up(r2a[p, 1, n]) + up(r2a[p, 2, n])).astype(BF)
-            t_b = (own_b + up(r2b[p, 0, n]) + up(r2b[p, 1, n]) + up(r2b[p, 2, n])).astype(BF)
-            cols = pl.ds(g * STEP, STEP)
-            s3[:, 0, :, cols] = nn(spread, t_a).astype(BF).reshape(DEPTH, 8, STEP)
-            s3[:, 1, :, cols] = nn(spread, t_b).astype(BF).reshape(DEPTH, 8, STEP)
+    for k in (1, 2, 3):
+        second_a(k).wait()
+        second_b(k).wait()
+    for g in range(1, GROUPS):
+        own_a = up(dw[g, 0, x, y]) + up(r1a[g, 0, y]) + up(r1a[g, 1, y]) + up(r1a[g, 2, y])
+        own_b = up(dw[g, 1, x, y]) + up(r1b[g, 0, x]) + up(r1b[g, 1, x]) + up(r1b[g, 2, x])
+        t_a = (own_a + up(r2a[0, g - 1]) + up(r2a[1, g - 1]) + up(r2a[2, g - 1])).astype(BF)
+        t_b = (own_b + up(r2b[0, g - 1]) + up(r2b[1, g - 1]) + up(r2b[2, g - 1])).astype(BF)
+        cols = pl.ds((g - 1) * STEP, STEP)
+        s3[:, 0, :, cols] = nn(spread, t_a).astype(BF).reshape(DEPTH, 8, STEP)
+        s3[:, 1, :, cols] = nn(spread, t_b).astype(BF).reshape(DEPTH, 8, STEP)
 
     def third(k):
         zp = lax.rem(level + k, DEPTH)
@@ -368,6 +369,23 @@
 
     for k in (4, 3, 5, 2, 6, 1, 7):
         third(k).start()
+
+    each(1, DEPTH, lambda k: level_first(k).wait())
+
+    def sum_levels(i):
+        for n in range(2):
+            part = up(zs[level, n, i])
+            for k in range(1, DEPTH):
+                part = part + up(zr[k, n, i])
+            zt[i, n] = part.astype(BF)
+
+    each(0, PEERS, sum_levels)
+
+    def plane_last(i, peer):
+        return remote(zt.at[peer], zu.at[i], tsend.at[i], trecv.at[i], seq=peer)
+
+    for i in range(1, PEERS):
+        plane_last(i, plane_peer(x, y, i)).start()
 
     place = lax.broadcasted_iota(jnp.int32, (OWNED * HALF, 2 * HALF), 0)
     slot = lax.broadcasted_iota(jnp.int32, (OWNED * HALF, 2 * HALF), 1)
@@ -391,8 +409,13 @@
     final = up(s3[level])
     for k in range(1, DEPTH):
         final = final + up(r3[k])
-    gw_ref[:, 0, :] = final[0, :PIECE]
-    gw_ref[:, 1, :] = final[1, :PIECE]
+    each(1, PEERS, lambda i: plane_last(i, after).wait())
+    zero = up(zt[me])
+    for i in range(1, PEERS):
+        zero = zero + up(zu[i])
+    for n in range(2):
+        gw_ref[:, n, pl.ds(0, STEP)] = zero[n, :PIECE]
+        gw_ref[:, n, pl.ds(STEP, FEAT - STEP)] = final[n, :PIECE]
 
     each(1, PEERS, lambda i: ask(i, after).wait_send())
     each(1, PEERS, lambda i: share_rows(i).wait_send())
@@ -402,18 +425,10 @@
     back.wait()
 
 
-def finish_kernel(gq, ge, gw, gq_out, ge_out, gw_out, sems):
-    copies = [pltpu.make_async_copy(gw, gw_out, sems.at[0])]
-    for n in range(4):
-        two = pl.ds(2 * n, 2)
-        copies.append(pltpu.make_async_copy(ge.at[two], ge_out.at[two], sems.at[1 + n]))
-    for n in range(2):
-        rows = pl.ds(n * ROWS // 2, ROWS // 2)
-        copies.append(pltpu.make_async_copy(gq.at[rows], gq_out.at[rows], sems.at[5 + n]))
-    for c in copies:
-        c.start()
-    for c in copies:
-        c.wait()
+def finish_kernel(gq, ge, gw, gq_out, ge_out, gw_out):
+    gq_out[...] = gq[...]
+    ge_out[...] = ge[...]
+    gw_out[...] = gw[...]
 
 
 def body(queries, out_grad, encodings, owner_map, nbr_count, key_weight, value_weight):
@@ -459,34 +474,43 @@
             bf(GROUPS, 2, SIDE, SIDE, SHARE, STEP),
             bf(GROUPS, SIDE - 1, SIDE, SHARE, STEP),
             bf(GROUPS, SIDE - 1, SIDE, SHARE, STEP),
-            bf(GROUPS // 2, 2, SIDE, SHARE, STEP),
-            bf(GROUPS // 2, 2, SIDE, SHARE, STEP),
-            bf(GROUPS // 2, SIDE - 1, 2, SHARE, STEP),
-            bf(GROUPS // 2, SIDE - 1, 2, SHARE, STEP),
-            bf(DEPTH, 2, 8, FEAT),
-            bf(DEPTH, 2, 8, FEAT),
+            bf(GROUPS - 1, SIDE, SHARE, STEP),
+            bf(GROUPS - 1, SIDE, SHARE, STEP),
+            bf(SIDE - 1, GROUPS - 1, SHARE, STEP),
+            bf(SIDE - 1, GROUPS - 1, SHARE, STEP),
+            bf(DEPTH, 2, 8, FEAT - STEP),
+            bf(DEPTH, 2, 8, FEAT - STEP),
+            bf(DEPTH, 2, PEERS, 8, STEP),
+            bf(DEPTH, 2, PEERS, 8, STEP),
+            bf(PEERS, 2, 8, STEP),
+            bf(PEERS, 2, 8, STEP),
             dma((6,)), dma((2,)),
             dma((PEERS,)), dma((PEERS,)), dma((PEERS,)), dma((PEERS,)), dma((PEERS,)), dma((PEERS,)),
             dma((2,)), dma((2,)), dma((2,)),
             dma((PEERS,)), dma((PEERS,)), dma((2,)), dma((2,)),
             dma((GROUPS, 3)), dma((GROUPS, 3)), dma((GROUPS, 3)), dma((GROUPS, 3)),
-            dma((2, 3)), dma((2, 3)), dma((2, 3)), dma((2, 3)),
-            dma((DEPTH,)), dma((DEPTH,)),
+            dma((3,)), dma((3,)), dma((3,)), dma((3,)),
+            dma((DEPTH,)), dma((DEPTH,)), dma((DEPTH,)), dma((DEPTH,)), dma((PEERS,)), dma((PEERS,)),
         ],
         compiler_params=pltpu.CompilerParams(
             collective_id=0, has_side_effects=True, vmem_limit_bytes=VMEM_LIMIT
         ),
         name="spans",
     )(
-        owner_map, nbr_count, encodings.reshape(OWNED, NROWS, D_ENC),
+        jnp.swapaxes(owner_map, 1, 2), nbr_count, encodings.reshape(OWNED, NROWS, D_ENC),
         queries[0], out_grad[0], key_weight, value_weight,
+    )
+    parts = (
+        pl.BlockSpec((ROWS // 4, FEAT), lambda n: (n, 0)),
+        pl.BlockSpec((OWNED // 4, NROWS, D_ENC), lambda n: (n, 0, 0)),
+        pl.BlockSpec((PIECE, 2, FEAT), lambda n: (0, 0, 0)),
     )
     gq, ge, gw = pl.pallas_call(
         finish_kernel,
+        grid=(4,),
         out_shape=tuple(jax.ShapeDtypeStruct(a.shape, a.dtype) for a in (gq, ge, gw)),
-        in_specs=[hbm] * 3,
-        out_specs=(hbm,) * 3,
-        scratch_shapes=[dma((7,))],
+        in_specs=parts,
+        out_specs=parts,
         name="finish",
     )(gq, ge, gw)
     return gq[None], ge.reshape(1, OWNED * NROWS, D_ENC), gw

time: 187 us -> 111 us (0.59)
  Pallas kernels: 185 us -> 110 us
    pallas_call x1, Pallas kernels: 74.4 us -> 3.93 us  [body(): pl.pallas_call(finish_kernel, grid=(4,), out_shape=tuple((jax.ShapeDtypeS...]
    pallas_call x1, Pallas kernels: 110 us -> 106 us  [body(): pl.pallas_call(kernel, out_shape=(jax.ShapeDtypeStruct((ROWS, FEAT), BF),...]
where the time goes in v4:
time: 111 us
  Pallas kernels  110 us (99%)
    pallas_call x1, Pallas kernels, body(): pl.pallas_call(kernel, out_shape=(jax.ShapeDtypeStruct((ROWS, FEAT), BF),...  106 us
    pallas_call x1, Pallas kernels, body(): pl.pallas_call(finish_kernel, grid=(4,), out_shape=tuple((jax.ShapeDtypeS...  3.93 us

profile of v4, /device:TPU:1, one launch (start us, length us, event | category | flops | bytes accessed | tf_op | source)
XLA Modules:
  0.0 110.8 jit_solution(16206186547647519193)
XLA Ops:
  0.6 106.2 %spans.1 = (bf16[256,1024]{1,0:T(8,128)(2,1)}, bf16[8,128,896]{2,1,0:T(8,128)(2,1)}, f32[7,2,1024]{2,1,0:T(2,128)}) custom-call(s32[1,2,4]{2,1,0:T(2,128)} %bitcast.9, s32[1,4]{1,0:T(1,128)} %cnt_ref.1, bf16[8,128,896]{2,1,0:T(8,128)(2,1)} %bitcast.6, bf16[256,1024]{1,0:T(8,128)(2,1)} %bitcast.7, bf16[256,1024]{1,0:T(8,128)(2,1)} %bitcast.8, ...), custom_call_target="tpu_custom_call" | custom-call | tf_op jit(solution)/shard_map/spans/pallas_call | solution.py:443
  106.9 3.9 %finish.1 = (bf16[256,1024]{1,0:T(8,128)(2,1)}, bf16[8,128,896]{2,1,0:T(8,128)(2,1)}, f32[7,2,1024]{2,1,0:T(2,128)}) custom-call(bf16[256,1024]{1,0:T(8,128)(2,1)} %get-tuple-element.9.gq, bf16[8,128,896]{2,1,0:T(8,128)(2,1)} %get-tuple-element.10.ge, f32[7,2,1024]{2,1,0:T(2,128)} %get-tuple-element.11.gw), custom_call_target="tpu_custom_call" | custom-call | tf_op jit(solution)/shard_map/finish/pallas_call | solution.py:508

commit v5 on v4

--- a/solution.py
+++ b/solution.py
@@ -24,6 +24,8 @@
 RIM = 64
 STEP = 256
 GROUPS = FEAT // STEP
+Z_GROUP = 2
+XY_GROUPS = [0, 1, 3]
 SHARE = D_ENC // PEERS
 PIECE = SHARE // DEPTH
 VMEM_LIMIT = 58 << 20
@@ -244,13 +246,14 @@
         xp = lax.rem(x + k, SIDE)
         return remote(s2b.at[:, xp], r2b.at[k - 1], send2b.at[k - 1], recv2b.at[k - 1], seq=xp * SIDE + y)
 
-    def sum_first(g):
+    def sum_first(n):
+        g = n + lax.div(n, 2)
         for k in (1, 2, 3):
             first_a(g, k).wait()
             first_b(g, k).wait()
         for j in range(SIDE):
-            s2a[g - 1, j] = (up(dw[g, 0, x, j]) + up(r1a[g, 0, j]) + up(r1a[g, 1, j]) + up(r1a[g, 2, j])).astype(BF)
-            s2b[g - 1, j] = (up(dw[g, 1, j, y]) + up(r1b[g, 0, j]) + up(r1b[g, 1, j]) + up(r1b[g, 2, j])).astype(BF)
+            s2a[n, j] = (up(dw[g, 0, x, j]) + up(r1a[g, 0, j]) + up(r1a[g, 1, j]) + up(r1a[g, 2, j])).astype(BF)
+            s2b[n, j] = (up(dw[g, 1, j, y]) + up(r1b[g, 0, j]) + up(r1b[g, 1, j]) + up(r1b[g, 2, j])).astype(BF)
 
     m = lax.broadcasted_iota(jnp.int32, (DEPTH * 8, SHARE), 0)
     e = lax.broadcasted_iota(jnp.int32, (DEPTH * 8, SHARE), 1)
@@ -260,7 +263,11 @@
         zp = lax.rem(level + k, DEPTH)
         return remote(zs.at[zp], zr.at[k], zsend.at[k], zrecv.at[k], dp=zp)
 
-    def group(g, first=False):
+    def halo_cols(g):
+        cols = pl.ds(pl.multiple_of(g * STEP, STEP), STEP)
+        return remote(gs.at[pl.ds(ROWS - RIM, RIM), cols], prev.at[:, cols], prev_sem.at[0, g], prev_sem.at[1, g], seq=after)
+
+    def group(g):
         cols = pl.ds(pl.multiple_of(g * STEP, STEP), STEP)
         cols_v = pl.ds(pl.multiple_of(g * STEP + FEAT, STEP), STEP)
         qs = nn(move, qx[:, cols]).astype(BF)
@@ -298,23 +305,32 @@
             dkv[two, :, head(h, FEAT)] = tn(pb, d).astype(BF).reshape(2, NROWS, HD)
         dk = dkv[:, :, cols].reshape(REFS * NROWS, STEP)
         dv = dkv[:, :, cols_v].reshape(REFS * NROWS, STEP)
+        plane = g != Z_GROUP
+        halo_cols(g).start()
         dw[g, 0] = nn(refs_t[...], dk).astype(BF).reshape(SIDE, SIDE, SHARE, STEP)
+
+        @pl.when(plane)
+        def _():
+            for k in (2, 1, 3):
+                first_a(g, k).start()
+
         dw[g, 1] = nn(refs_t[...], dv).astype(BF).reshape(SIDE, SIDE, SHARE, STEP)
-        if first:
+
+        @pl.when(plane)
+        def _():
+            for k in (2, 1, 3):
+                first_b(g, k).start()
+
+        @pl.when(jnp.logical_not(plane))
+        def _():
             for n in range(2):
                 for i in range(PEERS):
-                    zs[:, n, i] = nn(spread, dw[0, n, i // SIDE, i % SIDE]).astype(BF).reshape(DEPTH, 8, STEP)
+                    piece = nn(spread, dw[Z_GROUP, n, i // SIDE, i % SIDE])
+                    zs[:, n, i] = piece.astype(BF).reshape(DEPTH, 8, STEP)
             for k in (4, 3, 5, 2, 6, 1, 7):
                 level_first(k).start()
-        else:
-            for k in (2, 1, 3):
-                first_a(g, k).start()
-                first_b(g, k).start()
-
-    group(0, first=True)
-    each(1, GROUPS, group)
-    halo = remote(gs.at[pl.ds(ROWS - RIM, RIM)], prev, prev_sem.at[0], prev_sem.at[1], seq=after)
-    halo.start()
+
+    each(0, GROUPS, group)
 
     con[...] = nt(dkv[:, theirs, :].reshape(REFS * HALF, 2 * FEAT), w[...]).reshape(REFS, HALF, D_ENC)
     swap = remote(con, hbuf, swap_sem.at[0], swap_sem.at[1], head=other)
@@ -322,10 +338,6 @@
     own = nt(dkv[:, mine, :].reshape(REFS * HALF, 2 * FEAT), w[...]).reshape(REFS, HALF, D_ENC)
     swap.wait()
     half[...] = (own + hbuf[...]).astype(BF)
-    each(1, GROUPS, sum_first)
-    for k in (2, 1, 3):
-        second_a(k).start()
-        second_b(k).start()
 
     def ref_for(peer):
         found = jnp.int32(0)
@@ -338,13 +350,21 @@
     def return_rows(i, peer):
         return remote(send.at[i], recv.at[i], rsend.at[i], rrecv.at[i], seq=peer)
 
-    for i in range(1, PEERS):
+    for i in range(1, 9):
         peer = plane_peer(x, y, i)
         send[i] = half[ref_for(peer)]
         return_rows(i, peer).start()
     recv[0] = half[ref_for(me)]
-
-    halo.wait()
+    each(0, GROUPS - 1, sum_first)
+    for k in (2, 1, 3):
+        second_a(k).start()
+        second_b(k).start()
+    for i in range(9, PEERS):
+        peer = plane_peer(x, y, i)
+        send[i] = half[ref_for(peer)]
+        return_rows(i, peer).start()
+
+    each(0, GROUPS, lambda g: halo_cols(g).wait())
     old = jnp.where(me == 0, 0.0, 1.0)
     ext = jnp.concatenate([(up(prev[...]) * old).astype(BF), gs[...]], axis=0)
     gqv[...] = nn(shift_matrix(ROWS, ROWS + RIM, 1), ext).astype(BF)
@@ -354,12 +374,12 @@
     for k in (1, 2, 3):
         second_a(k).wait()
         second_b(k).wait()
-    for g in range(1, GROUPS):
+    for n, g in enumerate(XY_GROUPS):
         own_a = up(dw[g, 0, x, y]) + up(r1a[g, 0, y]) + up(r1a[g, 1, y]) + up(r1a[g, 2, y])
         own_b = up(dw[g, 1, x, y]) + up(r1b[g, 0, x]) + up(r1b[g, 1, x]) + up(r1b[g, 2, x])
-        t_a = (own_a + up(r2a[0, g - 1]) + up(r2a[1, g - 1]) + up(r2a[2, g - 1])).astype(BF)
-        t_b = (own_b + up(r2b[0, g - 1]) + up(r2b[1, g - 1]) + up(r2b[2, g - 1])).astype(BF)
-        cols = pl.ds((g - 1) * STEP, STEP)
+        t_a = (own_a + up(r2a[0, n]) + up(r2a[1, n]) + up(r2a[2, n])).astype(BF)
+        t_b = (own_b + up(r2b[0, n]) + up(r2b[1, n]) + up(r2b[2, n])).astype(BF)
+        cols = pl.ds(n * STEP, STEP)
         s3[:, 0, :, cols] = nn(spread, t_a).astype(BF).reshape(DEPTH, 8, STEP)
         s3[:, 1, :, cols] = nn(spread, t_b).astype(BF).reshape(DEPTH, 8, STEP)
 
@@ -396,10 +416,14 @@
         target = jnp.where(slot < HALF, slot + lo, slot - HALF + hi)
         live = jnp.where(slot < HALF, lo, hi) >= 0
         pick.append(jnp.logical_and(place == target, live).astype(F32).astype(BF))
-    pick = jnp.concatenate(pick, axis=1)
-    each(1, PEERS, lambda i: return_rows(i, after).wait_recv())
-    total = nn(pick, recv[...].reshape(PEERS * HALF, D_ENC))
-    ohalf[...] = total.astype(BF).reshape(OWNED, HALF, D_ENC)
+    early = PEERS // 2
+    each(1, early, lambda i: return_rows(i, after).wait_recv())
+    con[...] = nn(
+        jnp.concatenate(pick[: early // 2], axis=1), recv[:early].reshape(early * HALF, D_ENC)
+    ).reshape(OWNED, HALF, D_ENC)
+    each(early, PEERS, lambda i: return_rows(i, after).wait_recv())
+    late = nn(jnp.concatenate(pick[early // 2 :], axis=1), recv[early:].reshape(early * HALF, D_ENC))
+    ohalf[...] = (con[...] + late.reshape(OWNED, HALF, D_ENC)).astype(BF)
     back = remote(ohalf, ge_hbm.at[:, mine], back_sem.at[0], back_sem.at[1], head=other)
     back.start()
     ge_out = pltpu.make_async_copy(ohalf, ge_hbm.at[:, mine], osem.at[1])
@@ -413,9 +437,10 @@
     zero = up(zt[me])
     for i in range(1, PEERS):
         zero = zero + up(zu[i])
-    for n in range(2):
-        gw_ref[:, n, pl.ds(0, STEP)] = zero[n, :PIECE]
-        gw_ref[:, n, pl.ds(STEP, FEAT - STEP)] = final[n, :PIECE]
+    for t in range(2):
+        gw_ref[:, t, pl.ds(Z_GROUP * STEP, STEP)] = zero[t, :PIECE]
+        for n, g in enumerate(XY_GROUPS):
+            gw_ref[:, t, pl.ds(g * STEP, STEP)] = final[t, :PIECE, n * STEP : (n + 1) * STEP]
 
     each(1, PEERS, lambda i: ask(i, after).wait_send())
     each(1, PEERS, lambda i: share_rows(i).wait_send())
@@ -487,7 +512,7 @@
             dma((6,)), dma((2,)),
             dma((PEERS,)), dma((PEERS,)), dma((PEERS,)), dma((PEERS,)), dma((PEERS,)), dma((PEERS,)),
             dma((2,)), dma((2,)), dma((2,)),
-            dma((PEERS,)), dma((PEERS,)), dma((2,)), dma((2,)),
+            dma((PEERS,)), dma((PEERS,)), dma((2,)), dma((2, GROUPS)),
             dma((GROUPS, 3)), dma((GROUPS, 3)), dma((GROUPS, 3)), dma((GROUPS, 3)),
             dma((3,)), dma((3,)), dma((3,)), dma((3,)),
             dma((DEPTH,)), dma((DEPTH,)), dma((DEPTH,)), dma((DEPTH,)), dma((PEERS,)), dma((PEERS,)),

time: 111 us -> 107 us (0.964)
  Pallas kernels: 110 us -> 106 us
    pallas_call x1, Pallas kernels: 106 us -> 102 us  [body(): pl.pallas_call(kernel, out_shape=(jax.ShapeDtypeStruct((ROWS, FEAT), BF),...]
where the time goes in v5:
time: 107 us
  Pallas kernels  106 us (99%)
    pallas_call x1, Pallas kernels, body(): pl.pallas_call(kernel, out_shape=(jax.ShapeDtypeStruct((ROWS, FEAT), BF),...  102 us
    pallas_call x1, Pallas kernels, body(): pl.pallas_call(finish_kernel, grid=(4,), out_shape=tuple((jax.ShapeDtypeS...  3.93 us

profile of v5, /device:TPU:1, one launch (start us, length us, event | category | flops | bytes accessed | tf_op | source)
XLA Modules:
  0.0 106.5 jit_solution(8871011298256608871)
XLA Ops:
  0.6 101.9 %spans.1 = (bf16[256,1024]{1,0:T(8,128)(2,1)}, bf16[8,128,896]{2,1,0:T(8,128)(2,1)}, f32[7,2,1024]{2,1,0:T(2,128)}) custom-call(s32[1,2,4]{2,1,0:T(2,128)} %bitcast.9, s32[1,4]{1,0:T(1,128)} %cnt_ref.1, bf16[8,128,896]{2,1,0:T(8,128)(2,1)} %bitcast.6, bf16[256,1024]{1,0:T(8,128)(2,1)} %bitcast.7, bf16[256,1024]{1,0:T(8,128)(2,1)} %bitcast.8, ...), custom_call_target="tpu_custom_call" | custom-call | tf_op jit(solution)/shard_map/spans/pallas_call | solution.py:468
  102.6 3.9 %finish.1 = (bf16[256,1024]{1,0:T(8,128)(2,1)}, bf16[8,128,896]{2,1,0:T(8,128)(2,1)}, f32[7,2,1024]{2,1,0:T(2,128)}) custom-call(bf16[256,1024]{1,0:T(8,128)(2,1)} %get-tuple-element.9.gq, bf16[8,128,896]{2,1,0:T(8,128)(2,1)} %get-tuple-element.10.ge, f32[7,2,1024]{2,1,0:T(2,128)} %get-tuple-element.11.gw), custom_call_target="tpu_custom_call" | custom-call | tf_op jit(solution)/shard_map/finish/pallas_call | solution.py:533
